TPU v7x, 32 devices: a whole 2x2x4 slice. The times are simulated.
32 devices in a mesh: fsdp: 2 (over x), ctx: 4 (over z), tp: 4 (over y, core).
Axes of the slice: x: 2, y: 2, z: 4, core: 2. Of those that a mesh axis runs over, the one named last changes fastest.
Arguments:
- frames_in: bfloat16 [4, 12544, 768], P(None, ('fsdp', 'ctx', 'tp')), may hold values from -6 to 6
- out_grad: bfloat16 [4, 12544, 768], P(None, ('fsdp', 'ctx', 'tp')), may hold values from -6 to 6
- w_query: bfloat16 [768, 768], P('fsdp', 'tp'), may hold values from -0.3125 to 0.3125
- w_key: bfloat16 [768, 768], P('fsdp', 'tp'), may hold values from -0.3125 to 0.3125
- w_value: bfloat16 [768, 768], P('fsdp', 'tp'), may hold values from -0.21875 to 0.21875
- w_out: bfloat16 [768, 768], P('tp', 'fsdp'), may hold values from -1.5 to 1.5
- w_up: bfloat16 [768, 3072], P('fsdp', 'tp'), may hold values from -0.21875 to 0.21875
- w_down: bfloat16 [3072, 768], P('tp', 'fsdp'), may hold values from -0.109375 to 0.109375
- norm1_gain: bfloat16 [768], P('fsdp'), may hold values from 0.5 to 1.5
- norm1_bias: bfloat16 [768], P('fsdp'), may hold values from -3 to 3
- norm2_gain: bfloat16 [768], P('fsdp'), may hold values from 0.5 to 1.5
- norm2_bias: bfloat16 [768], P('fsdp'), may hold values from -3 to 3
Outputs:
- block_out: bfloat16 [4, 12544, 768], P(None, ('fsdp', 'ctx', 'tp'))
- input_grad: float32 [4, 12544, 768], P(None, ('fsdp', 'ctx', 'tp'))
- grad_query: float32 [768, 768], P('fsdp', 'tp')
- grad_key: float32 [768, 768], P('fsdp', 'tp')
- grad_value: float32 [768, 768], P('fsdp', 'tp')
- grad_out: float32 [768, 768], P('tp', 'fsdp')
- grad_up: float32 [768, 3072], P('fsdp', 'tp')
- grad_down: float32 [3072, 768], P('tp', 'fsdp')
- grad_norm1_gain: float32 [768], P('fsdp')
- grad_norm1_bias: float32 [768], P('fsdp')
- grad_norm2_gain: float32 [768], P('fsdp')
- grad_norm2_bias: float32 [768], P('fsdp')
All inputs are finite; a program needn't handle non-finite values.
Results may differ from a plain program's by a relative error of at most 0.012.
The roundings to bfloat16 on the way count: a program that leaves them out, or rounds other values in their place, can miss the bound.
Values may be sent and summed in bfloat16 or wider, within the bound.
No kernel may reach another device: no remote copies, remote signals or barrier semaphores. Data moves between devices by JAX's collectives and lax.ppermute only.
A program may use at most 128 MiB of HBM per device.

v0:
```python
import functools
import math

import jax
import jax.numpy as jnp
from jax import lax
from jax.experimental import pallas as pl
from jax.experimental.pallas import tpu as pltpu
from jax.sharding import PartitionSpec as P


HEADS = 12
PLACES = 196
PADDED = 208

EPSILON = 1e-06
INV_ROOT_TWO = 0.7071067811865476
INV_ROOT_TAU = 0.3989422804014327
LOWEST = -1e30

VMEM_BYTES = 60 * 1024 * 1024


def dot_rows(left, right):
    return lax.dot_general(
        left, right, (((1,), (0,)), ((), ())), preferred_element_type=jnp.float32
    )


def dot_right_t(left, right):
    return lax.dot_general(
        left, right, (((1,), (1,)), ((), ())), preferred_element_type=jnp.float32
    )


def dot_left_t(left, right):
    return lax.dot_general(
        left, right, (((0,), (0,)), ((), ())), preferred_element_type=jnp.float32
    )


def standardize_rows(rows_in):
    center = rows_in - jnp.mean(rows_in, axis=-1, keepdims=True)
    spread = jnp.mean(center * center, axis=-1, keepdims=True)
    reciprocal_spread = lax.rsqrt(spread + EPSILON)
    return (center * reciprocal_spread, reciprocal_spread)


def norm_backward_pass(norm_gradient, gain_vector, centered_rows, reciprocal_spread):
    scaled_result = norm_gradient * gain_vector
    leading_part = jnp.mean(scaled_result, axis=-1, keepdims=True)
    trailing_part = jnp.mean(scaled_result * centered_rows, axis=-1, keepdims=True)
    return reciprocal_spread * (scaled_result - leading_part - centered_rows * trailing_part)


def swap(block, axis, mask):
    count = lax.axis_size(axis)
    return lax.ppermute(block, axis, [(i, i ^ mask) for i in range(count)])


def bits_of(axis):
    return [(axis, 1 << b) for b in reversed(range(lax.axis_size(axis).bit_length() - 1))]


def orders():
    along_f, along_t = bits_of("fsdp"), bits_of("tp")
    first, last = along_t[:-1], along_t[-1:]
    return (along_f + first + last, first + along_f + last)


def piece_masks():
    masks = [0]
    for _, mask in bits_of("tp"):
        masks = [m for m in masks] + [m ^ mask for m in masks]
    return masks


class Pack:
    def __init__(self, arrays, pieces, part):
        self.arrays, self.pieces, self.part = arrays, pieces, part

    def copies(self, refs, piece, first, count, target, row):
        mine = lax.axis_index("fsdp")
        made = []
        for array, start, rows, place, mask in self.pieces[piece]:
            low, high = max(first, place), min(first + count, place + rows)
            if low >= high:
                continue
            source = refs[array].at[pl.ds(start + low - place, high - low), :]
            where = pl.ds(row + low - first, high - low)
            if mask is None:
                made.append((source, target.at[where, :]))
            else:
                column = pl.multiple_of((mine ^ mask) * self.part, 128)
                made.append((source, target.at[where, pl.ds(column, self.part)]))
        return made


def start_copies(pairs, sems, at):
    made = [
        pltpu.make_async_copy(source, target, sems.at[at + n])
        for n, (source, target) in enumerate(pairs)
    ]
    for copy in made:
        copy.start()
    return made


def gather_pack(block):
    f_count, t_count = lax.axis_size("fsdp"), lax.axis_size("tp")
    rows, part = block.shape
    if f_count == 2 and t_count == 4 and part % 128 == 0:
        half = rows // 2
        beside_f = swap(block, "fsdp", 1)
        beside_t = swap(block, "tp", 2)
        across = (swap(beside_f[:half], "tp", 2), swap(beside_t[half:], "fsdp", 1))
        here = (block, beside_f, beside_t) + across
        there = tuple(swap(array, "tp", 1) for array in here)
        pieces = []
        for base in (0, len(here)):
            pieces.append([(base, 0, rows, 0, 0), (base + 1, 0, rows, 0, 1)])
            pieces.append(
                [
                    (base + 2, 0, rows, 0, 0),
                    (base + 3, 0, half, 0, 1),
                    (base + 4, 0, half, half, 1),
                ]
            )
        return Pack(here + there, pieces, part)
    held, keys = block[None], [(0, 0)]
    for axis, mask in orders()[0]:
        held = jnp.concatenate([held, swap(held, axis, mask)], axis=0)
        keys = keys + [(f ^ mask, t) if axis == "fsdp" else (f, t ^ mask) for f, t in keys]
    place = {key: n for n, key in enumerate(keys)}
    mine = lax.axis_index("fsdp")
    full = []
    for t in piece_masks():
        stacked = jnp.stack([held[place[(f, t)]] for f in range(f_count)])
        parts = [
            lax.dynamic_index_in_dim(stacked, mine ^ f, 0, keepdims=False)
            for f in range(f_count)
        ]
        full.append(jnp.concatenate(parts, axis=1))
    pieces = [[(p, 0, rows, 0, None)] for p in range(t_count)]
    return Pack(tuple(full), pieces, part)


def gather_columns(block):
    held, masks = [block], [0]
    for axis, mask in bits_of("fsdp"):
        got = swap(jnp.stack(held), axis, mask)
        held = held + [got[n] for n in range(len(held))]
        masks = masks + [m ^ mask for m in masks]
    mine = lax.axis_index("fsdp")
    count = len(held)
    stacked = jnp.stack([held[masks.index(m)] for m in range(count)])
    parts = [
        lax.dynamic_index_in_dim(stacked, mine ^ m, 0, keepdims=False) for m in range(count)
    ]
    return jnp.concatenate(parts, axis=1)


def reduce_step(held, step, piece_axis, part_axis):
    axis, mask = step
    if axis == "tp":
        half = held.shape[piece_axis] // 2
        keep = lax.slice_in_dim(held, 0, half, axis=piece_axis)
        sent = lax.slice_in_dim(held, half, 2 * half, axis=piece_axis)
    else:
        part = held.shape[part_axis] // 2
        bit = jnp.where((lax.axis_index("fsdp") & mask) != 0, 1, 0)
        keep = lax.dynamic_slice_in_dim(held, bit * part, part, part_axis)
        sent = lax.dynamic_slice_in_dim(held, (1 - bit) * part, part, part_axis)
    return keep + swap(sent.astype(jnp.bfloat16), axis, mask).astype(jnp.float32)


def sum_over_ctx(block):
    count = lax.axis_size("ctx")
    bit = lax.axis_index("ctx") & 1
    rows = block.shape[0] // 2
    sent = lax.dynamic_slice_in_dim(block, (1 - bit) * rows, rows, 0)
    got = swap(sent.astype(jnp.bfloat16), "ctx", 1)
    held = lax.dynamic_slice_in_dim(block, bit * rows, rows, 0) + got.astype(jnp.float32)
    mask = 2
    while mask < count:
        got = swap(held.astype(jnp.bfloat16), "ctx", mask)
        held = held + got.astype(jnp.float32)
        mask *= 2
    other = swap(held.astype(jnp.bfloat16), "ctx", 1).astype(jnp.float32)
    return jnp.where(
        bit == 0,
        jnp.concatenate([held, other], axis=0),
        jnp.concatenate([other, held], axis=0),
    )


def sum_in_plane(block):
    for axis in ("tp", "fsdp"):
        for _, mask in reversed(bits_of(axis)):
            block = block + swap(block, axis, mask)
    return block


def params():
    return pltpu.CompilerParams(vmem_limit_bytes=VMEM_BYTES)


def cost(micros):
    return pl.CostEstimate(flops=int(micros * 1.1e9), bytes_accessed=0, transcendentals=0)


def whole(shape):
    return pl.BlockSpec(shape, lambda i: (0,) * len(shape), pipeline_mode=pl.Buffered(1))


def rows_of(count, width, column=0):
    return pl.BlockSpec((count, width), lambda i: (i, column))


def in_place(arrays):
    return [pl.BlockSpec(memory_space=pl.ANY)] * len(arrays)


def pad_kernel(count, x_ref, g_ref, xo_ref, go_ref):
    for source, target in ((x_ref, xo_ref), (g_ref, go_ref)):
        block = source[0].astype(jnp.float32)
        blank = jnp.zeros((PADDED - PLACES, block.shape[1]), jnp.float32)
        parts = []
        for n in range(count):
            parts += [block[n * PLACES : (n + 1) * PLACES], blank]
        target[...] = jnp.concatenate(parts, axis=0).astype(target.dtype)


def pack_near_kernel(q_ref, k_ref, v_ref, o_ref, out_ref):
    units = q_ref.shape[1]
    for n, ref in enumerate((q_ref, k_ref, v_ref)):
        out_ref[n * units : (n + 1) * units, :] = ref[...].T
    out_ref[3 * units :, :] = o_ref[...]


def pack_feed_kernel(up_ref, down_ref, gate_ref, out_ref):
    units = up_ref.shape[1]
    out_ref[:units, :] = up_ref[...].T
    out_ref[units:, :] = down_ref[...]


def unpad(block):
    count = block.shape[0] // PADDED
    return jnp.concatenate(
        [block[n * PADDED : n * PADDED + PLACES] for n in range(count)], axis=0
    )


def low_lanes(head_size):
    lane = lax.broadcasted_iota(jnp.int32, (1, 2 * head_size), 1)
    return lane < head_size


def projection_copies(pack, refs, units, target):
    pieces = len(pack.pieces)
    side = pieces // 2 * units
    made = []
    for p in range(pieces):
        half, place = divmod(p, pieces // 2)
        for kind in range(3):
            row = (half * 3 + kind) * side + place * units
            made += pack.copies(refs, p, kind * units, units, target, row)
    return made


def attend_kernel(heads, head_size, pack, units, *refs):
    count = len(pack.arrays)
    x_ref, norm_ref = refs[:2]
    raw = refs[2 : 2 + count]
    xn_ref, qkv_ref, mixed_ref, log_ref, hidden_ref, sn_ref = refs[2 + count : 8 + count]
    wqkv_ref, wout_ref, sems = refs[8 + count :]
    width = heads * head_size
    side = width // 2

    @pl.when(pl.program_id(0) == 0)
    def _():
        pairs = projection_copies(pack, raw, units, wqkv_ref)
        for p in range(len(pack.pieces)):
            pairs += pack.copies(raw, p, 3 * units, units, wout_ref, p * units)
        for copy in start_copies(pairs, sems, 0):
            copy.wait()

    tokens = x_ref[...].astype(jnp.float32)
    hat, _ = standardize_rows(tokens)
    normed = (hat * norm_ref[0:1, :] + norm_ref[1:2, :]).astype(jnp.bfloat16)
    xn_ref[...] = normed
    for part in range(6):
        cut = slice(part * side, (part + 1) * side)
        qkv_ref[:, cut] = dot_right_t(normed, wqkv_ref[cut, :]).astype(jnp.bfloat16)
    low_half = low_lanes(head_size)
    scale = 1.0 / math.sqrt(head_size)

    def one_frame(n, carry):
        rows = pl.ds(pl.multiple_of(n * PADDED, 16), PADDED)
        valid = lax.broadcasted_iota(jnp.int32, (1, PADDED), 1) < PLACES
        for pair in range(heads // 2):
            half, place = divmod(pair, heads // 4)
            at = 3 * half * side + place * 2 * head_size
            q2 = qkv_ref[rows, at : at + 2 * head_size] * jnp.bfloat16(scale)
            k2 = qkv_ref[rows, side + at : side + at + 2 * head_size]
            v2 = qkv_ref[rows, 2 * side + at : 2 * side + at + 2 * head_size]
            outs = []
            for hand in range(2):
                keep = low_half if hand == 0 else ~low_half
                q1 = jnp.where(keep, q2, jnp.zeros_like(q2))
                scores = jnp.where(valid, dot_right_t(q1, k2), LOWEST)
                top = jnp.max(scores, axis=-1, keepdims=True)
                powers = jnp.exp(scores - top)
                total = jnp.sum(powers, axis=-1, keepdims=True)
                log_ref[rows, 2 * pair + hand : 2 * pair + hand + 1] = top + jnp.log(total)
                probs = (powers * (1.0 / total)).astype(jnp.bfloat16)
                outs.append(dot_rows(probs, v2))
            mixed_ref[rows, 2 * pair * head_size : 2 * (pair + 1) * head_size] = jnp.where(
                low_half, outs[0], outs[1]
            ).astype(jnp.bfloat16)
        return carry

    lax.fori_loop(0, tokens.shape[0] // PADDED, one_frame, 0)
    hidden = tokens + dot_rows(mixed_ref[...], wout_ref[...])
    hidden_ref[...] = hidden
    hat2, _ = standardize_rows(hidden)
    sn_ref[...] = (hat2 * norm_ref[2:3, :] + norm_ref[3:4, :]).astype(jnp.bfloat16)


def forward_kernel(tile, pack, units, *refs):
    count = len(pack.arrays)
    sn_ref, cot_ref, snt_ref, cott_ref, hidden_ref, norm_ref = refs[:6]
    raw = refs[6 : 6 + count]
    out_ref, dh_ref, keep_ref, send_ref, ngrad_ref = refs[6 + count : 11 + count]
    y_ref, act_ref, din_ref, next_ref, wup_ref, wdown_ref, sems = refs[11 + count :]
    step, steps = pl.program_id(0), len(pack.pieces)
    tiles = sn_ref.shape[0] // tile

    def copies_of(p):
        pairs = pack.copies(raw, p, 0, units, next_ref.at[0], 0)
        pairs += pack.copies(raw, p, units, units, next_ref.at[1], 0)
        return [
            pltpu.make_async_copy(source, target, sems.at[n])
            for n, (source, target) in enumerate(pairs)
        ]

    @pl.when(step == 0)
    def _():
        for copy in copies_of(0):
            copy.start()
        y_ref[...] = jnp.zeros_like(y_ref)
        dh_ref[...] = jnp.zeros_like(dh_ref)

    for p in range(steps):

        @pl.when(step == p)
        def _(p=p):
            for copy in copies_of(p):
                copy.wait()
            wup_ref[...] = next_ref[0]
            wdown_ref[...] = next_ref[1]
            if p + 1 < steps:
                for copy in copies_of(p + 1):
                    copy.start()

    def one_tile(n, carry):
        rows = pl.ds(pl.multiple_of(n * tile, 16), tile)
        wup, wdown = wup_ref[...], wdown_ref[...]
        inner = dot_right_t(sn_ref[rows, :], wup)
        d_active = dot_right_t(cot_ref[rows, :], wdown)
        share = 0.5 * (1.0 + lax.erf(inner * INV_ROOT_TWO))
        active = (inner * share).astype(jnp.bfloat16)
        slope = share + inner * (jnp.exp(-0.5 * inner * inner) * INV_ROOT_TAU)
        d_inner = (d_active * slope).astype(jnp.bfloat16)
        act_ref[rows, :] = active
        din_ref[rows, :] = d_inner
        y_ref[rows, :] += dot_rows(active, wdown)
        dh_ref[rows, :] += dot_rows(d_inner, wup)
        return carry

    lax.fori_loop(0, tiles, one_tile, 0)

    @pl.when(step < steps // 2)
    def _():
        keep_ref[0, 0] = dot_rows(snt_ref[...], din_ref[...])
        keep_ref[0, 1] = dot_rows(cott_ref[...], act_ref[...])

    @pl.when(step >= steps // 2)
    def _():
        send_ref[0, 0] = dot_rows(snt_ref[...], din_ref[...]).astype(jnp.bfloat16)
        send_ref[0, 1] = dot_rows(cott_ref[...], act_ref[...]).astype(jnp.bfloat16)

    @pl.when(step == steps - 1)
    def _():
        ngrad_ref[...] = jnp.zeros_like(ngrad_ref)

        def close(n, carry):
            rows = pl.ds(pl.multiple_of(n * tile, 16), tile)
            hidden = hidden_ref[rows, :]
            out_ref[n] = unpad(hidden + y_ref[rows, :]).astype(jnp.bfloat16)
            hat2, scale2 = standardize_rows(hidden)
            d_second = dh_ref[rows, :]
            dh_ref[rows, :] = cot_ref[rows, :].astype(jnp.float32) + norm_backward_pass(
                d_second, norm_ref[2:3, :], hat2, scale2
            )
            ngrad_ref[2:3, :] += jnp.sum(d_second * hat2, axis=0, keepdims=True)
            ngrad_ref[3:4, :] += jnp.sum(d_second, axis=0, keepdims=True)
            return carry

        lax.fori_loop(0, tiles, close, 0)


def backward_kernel(heads, head_size, half, pack, units, *refs):
    count = len(pack.arrays)
    dh_ref, qkv_ref, log_ref = refs[:3]
    raw = refs[3 : 3 + count]
    dqkv_ref, dmix_ref, wout_ref, sems = refs[3 + count :]
    side = heads // 2 * head_size
    scale = 1.0 / math.sqrt(head_size)
    here = len(pack.pieces) // 2

    @pl.when(pl.program_id(0) == 0)
    def _():
        pairs = []
        for n in range(here):
            pairs += pack.copies(raw, half * here + n, 3 * units, units, wout_ref, n * units)
        for copy in start_copies(pairs, sems, 0):
            copy.wait()

    low = dh_ref[...].astype(jnp.bfloat16)
    dmix_ref[...] = dot_right_t(low, wout_ref[...]).astype(jnp.bfloat16)
    low_half = low_lanes(head_size)

    def one_frame(n, carry):
        rows = pl.ds(pl.multiple_of(n * PADDED, 16), PADDED)
        valid = lax.broadcasted_iota(jnp.int32, (1, PADDED), 1) < PLACES
        for pair in range(heads // 4):
            at = pair * 2 * head_size
            q2 = qkv_ref[rows, at : at + 2 * head_size]
            qs = q2 * jnp.bfloat16(scale)
            k2 = qkv_ref[rows, side + at : side + at + 2 * head_size]
            v2 = qkv_ref[rows, 2 * side + at : 2 * side + at + 2 * head_size]
            g2 = dmix_ref[rows, at : at + 2 * head_size]
            dq, dk, dv = [], [], []
            for hand in range(2):
                keep = low_half if hand == 0 else ~low_half
                q1 = jnp.where(keep, qs, jnp.zeros_like(qs))
                g1 = jnp.where(keep, g2, jnp.zeros_like(g2))
                scores = jnp.where(valid, dot_right_t(q1, k2), LOWEST)
                head = half * (heads // 2) + 2 * pair + hand
                probs = jnp.exp(scores - log_ref[rows, head : head + 1])
                probs_low = probs.astype(jnp.bfloat16)
                d_probs = dot_right_t(g1, v2)
                delta = jnp.sum(d_probs * probs, axis=-1, keepdims=True)
                d_scores = (probs * (d_probs - delta)).astype(jnp.bfloat16)
                dv.append(dot_left_t(probs_low, g2))
                dq.append(dot_rows(d_scores, k2))
                dk.append(dot_left_t(d_scores, q2))
            for part, pieces, factor in ((0, dq, scale), (1, dk, scale), (2, dv, 1.0)):
                dqkv_ref[rows, part * side + at : part * side + at + 2 * head_size] = (
                    jnp.where(low_half, pieces[0], pieces[1]) * factor
                ).astype(jnp.bfloat16)
        return carry

    lax.fori_loop(0, low.shape[0] // PADDED, one_frame, 0)


def input_kernel(pack, units, *refs):
    count = len(pack.arrays)
    x_ref, dh_ref, first_ref, last_ref, norm_ref = refs[:5]
    raw = refs[5 : 5 + count]
    grad_ref, ngrad_ref, wqkv_ref, sems = refs[5 + count :]
    side = first_ref.shape[1]

    @pl.when(pl.program_id(0) == 0)
    def _():
        ngrad_ref[...] = jnp.zeros_like(ngrad_ref)
        for copy in start_copies(projection_copies(pack, raw, units, wqkv_ref), sems, 0):
            copy.wait()

    d_first = dot_rows(first_ref[...], wqkv_ref[:side, :])
    d_first += dot_rows(last_ref[...], wqkv_ref[side:, :])
    hat1, scale1 = standardize_rows(x_ref[...].astype(jnp.float32))
    grad_ref[0] = unpad(
        dh_ref[...] + norm_backward_pass(d_first, norm_ref[0:1, :], hat1, scale1)
    )
    ngrad_ref[0:1, :] += jnp.sum(d_first * hat1, axis=0, keepdims=True)
    ngrad_ref[1:2, :] += jnp.sum(d_first, axis=0, keepdims=True)


def on_device(
    frames_in,
    out_grad,
    w_query,
    w_key,
    w_value,
    w_out,
    w_up,
    w_down,
    norm1_gain,
    norm1_bias,
    norm2_gain,
    norm2_bias,
):
    block_count, resident_rows, width = frames_in.shape
    frames_each = resident_rows // PLACES
    block_rows = frames_each * PADDED
    rows = block_count * block_rows
    head_size = width // HEADS
    units = w_query.shape[1]
    part = w_query.shape[0]
    hidden_units = w_up.shape[1]
    order_a, order_b = orders()
    pieces = lax.axis_size("tp")
    low, full = jnp.bfloat16, jnp.float32
    sds = jax.ShapeDtypeStruct

    near = pl.pallas_call(
        pack_near_kernel,
        name="pack_near",
        out_shape=sds((4 * units, part), low),
        compiler_params=params(),
    )(w_query, w_key, w_value, w_out)
    attention = gather_pack(near)
    norms_here = jnp.stack([norm1_gain, norm1_bias, norm2_gain, norm2_bias])
    norms_here = jnp.pad(norms_here, ((0, 4), (0, 0)))
    norms = gather_columns(norms_here).astype(full)
    feed_here = pl.pallas_call(
        pack_feed_kernel,
        name="pack_feed",
        in_specs=[pl.BlockSpec(memory_space=pltpu.VMEM)] * 2 + [pl.BlockSpec(memory_space=pl.ANY)],
        out_shape=sds((2 * hidden_units, part), low),
        compiler_params=params(),
    )(w_up, w_down, attention.arrays[1])
    feed = gather_pack(feed_here)

    resident = pl.BlockSpec((1, resident_rows, width), lambda i: (i, 0, 0))
    tokens, cotangent = pl.pallas_call(
        functools.partial(pad_kernel, frames_each),
        name="pad_frames",
        grid=(block_count,),
        in_specs=[resident, resident],
        out_specs=[rows_of(block_rows, width)] * 2,
        out_shape=[sds((rows, width), low)] * 2,
        compiler_params=params(),
        cost_estimate=cost(5),
    )(frames_in, out_grad)

    normed, qkv, mixed, logs, hidden, second = pl.pallas_call(
        functools.partial(attend_kernel, HEADS, head_size, attention, units),
        name="attend",
        grid=(block_count,),
        in_specs=[rows_of(block_rows, width), whole((8, width))]
        + in_place(attention.arrays),
        out_specs=[
            rows_of(block_rows, width),
            rows_of(block_rows, 3 * width),
            rows_of(block_rows, width),
            rows_of(block_rows, 128),
            rows_of(block_rows, width),
            rows_of(block_rows, width),
        ],
        out_shape=[
            sds((rows, width), low),
            sds((rows, 3 * width), low),
            sds((rows, width), low),
            sds((rows, 128), full),
            sds((rows, width), full),
            sds((rows, width), low),
        ],
        scratch_shapes=[
            pltpu.VMEM((3 * width, width), low),
            pltpu.VMEM((width, width), low),
            pltpu.SemaphoreType.DMA((64,)),
        ],
        compiler_params=params(),
        cost_estimate=cost(30),
    )(tokens, norms, *attention.arrays)

    half = pieces // 2
    keep_block = pl.BlockSpec(
        (1, 2, width, hidden_units), lambda i: (jnp.minimum(i, half - 1), 0, 0, 0)
    )
    send_block = pl.BlockSpec(
        (1, 2, width, hidden_units), lambda i: (jnp.maximum(i - half, 0), 0, 0, 0)
    )
    block_out, d_hidden, feed_keep, feed_send, second_terms = pl.pallas_call(
        functools.partial(forward_kernel, block_rows, feed, hidden_units),
        name="feed_forward",
        grid=(pieces,),
        in_specs=[
            whole((rows, width)),
            whole((rows, width)),
            whole((width, rows)),
            whole((width, rows)),
            whole((rows, width)),
            whole((8, width)),
        ]
        + in_place(feed.arrays),
        out_specs=[
            whole(frames_in.shape),
            whole((rows, width)),
            keep_block,
            send_block,
            whole((8, width)),
        ],
        out_shape=[
            sds(frames_in.shape, low),
            sds((rows, width), full),
            sds((half, 2, width, hidden_units), full),
            sds((half, 2, width, hidden_units), low),
            sds((8, width), full),
        ],
        scratch_shapes=[
            pltpu.VMEM((rows, width), full),
            pltpu.VMEM((rows, hidden_units), low),
            pltpu.VMEM((rows, hidden_units), low),
            pltpu.VMEM((2, hidden_units, width), low),
            pltpu.VMEM((hidden_units, width), low),
            pltpu.VMEM((hidden_units, width), low),
            pltpu.SemaphoreType.DMA((16,)),
        ],
        compiler_params=params(),
        cost_estimate=cost(62),
    )(second, cotangent, second.T, cotangent.T, hidden, norms, *feed.arrays)

    last = order_a[-1]
    steps_a, steps_b = order_a[:-1][::-1], order_b[:-1][::-1]
    feed_got = swap(feed_send, *last)
    out_total = dot_left_t(mixed, d_hidden.astype(low))
    up_held = feed_keep[:, 0] + feed_got[:, 0].astype(full)
    down_held = feed_keep[:, 1] + feed_got[:, 1].astype(full)

    def attention_back(side):
        wide = 3 * width // 2
        return pl.pallas_call(
            functools.partial(backward_kernel, HEADS, head_size, side, attention, units),
            grid=(block_count,),
            in_specs=[
                rows_of(block_rows, width),
                rows_of(block_rows, wide, side),
                rows_of(block_rows, 128),
            ]
            + in_place(attention.arrays),
            out_specs=rows_of(block_rows, wide),
            out_shape=sds((rows, wide), low),
            scratch_shapes=[
                pltpu.VMEM((block_rows, width // 2), low),
                pltpu.VMEM((width // 2, width), low),
                pltpu.SemaphoreType.DMA((16,)),
            ],
            compiler_params=params(),
            cost_estimate=cost(25),
        )(d_hidden, qkv, logs, *attention.arrays)

    side = width // 2
    d_last = attention_back(1)
    last_total = dot_left_t(d_last, normed)
    near_send = jnp.concatenate([last_total, out_total[side:]], axis=0).astype(low)
    near_got = swap(near_send, *last)
    d_lead = attention_back(0)
    for step_a, step_b in zip(steps_a, steps_b):
        up_held = reduce_step(up_held, step_a, 0, 1)
        down_held = reduce_step(down_held, step_b, 0, 1)
    feed_sum = sum_over_ctx(jnp.concatenate([up_held[0], down_held[0]], axis=0))

    lead_total = dot_left_t(d_lead, normed)
    shape = (2, half, units, width)
    a_held = lead_total[: 2 * side] + near_got[: 2 * side].astype(full)
    b_held = jnp.concatenate([lead_total[2 * side :], out_total[:side]], axis=0) + near_got[
        2 * side :
    ].astype(full)
    a_held, b_held = a_held.reshape(shape), b_held.reshape(shape)

    wide = 3 * width // 2
    input_grad, first_terms = pl.pallas_call(
        functools.partial(input_kernel, attention, units),
        name="input_gradient",
        grid=(block_count,),
        in_specs=[
            rows_of(block_rows, width),
            rows_of(block_rows, width),
            rows_of(block_rows, wide),
            rows_of(block_rows, wide),
            whole((8, width)),
        ]
        + in_place(attention.arrays),
        out_specs=[resident, whole((8, width))],
        out_shape=[sds(frames_in.shape, full), sds((8, width), full)],
        scratch_shapes=[
            pltpu.VMEM((3 * width, width), low),
            pltpu.SemaphoreType.DMA((64,)),
        ],
        compiler_params=params(),
        cost_estimate=cost(14),
    )(tokens, d_hidden, d_lead, d_last, norms, *attention.arrays)

    for step_a, step_b in zip(steps_a, steps_b):
        a_held = reduce_step(a_held, step_a, 1, 3)
        b_held = reduce_step(b_held, step_b, 1, 3)
    norm_terms = sum_in_plane(
        jnp.where(
            lax.broadcasted_iota(jnp.int32, first_terms.shape, 0) < 2, first_terms, second_terms
        ),
    )
    norm_terms = lax.dynamic_slice_in_dim(
        norm_terms, lax.axis_index("fsdp") * part, part, 1
    )
    norm_terms = jnp.pad(norm_terms, ((0, 8), (0, 0)))
    near_sum = sum_over_ctx(
        jnp.concatenate(
            [a_held.reshape(-1, part), b_held.reshape(-1, part), norm_terms], axis=0
        ),
    )
    base = 4 * units
    return (
        block_out,
        input_grad,
        near_sum[:units].T,
        near_sum[units : 2 * units].T,
        near_sum[2 * units : 3 * units].T,
        near_sum[3 * units : base],
        feed_sum[:part],
        feed_sum[part:].T,
        near_sum[base],
        near_sum[base + 1],
        near_sum[base + 2],
        near_sum[base + 3],
    )


def solution(mesh):
    tokens = P(None, ("fsdp", "ctx", "tp"), None)
    weights = (
        P("fsdp", "tp"),
        P("fsdp", "tp"),
        P("fsdp", "tp"),
        P("tp", "fsdp"),
        P("fsdp", "tp"),
        P("tp", "fsdp"),
        P("fsdp"),
        P("fsdp"),
        P("fsdp"),
        P("fsdp"),
    )
    return jax.shard_map(
        on_device,
        mesh=mesh,
        in_specs=(tokens, tokens) + weights,
        out_specs=(tokens, tokens) + weights,
        check_vma=False,
    )
```

profile of v0, /device:TPU:0, one launch (start us, length us, event | category | flops | bytes accessed | tf_op | source)
XLA Modules:
  0.0 432.1 jit_solution(12598129191665593287)
XLA Ops:
  8.1 3.0 collective-permute-start.1
  11.1 13.5 %collective-permute-done.1.refs_3_.gate_ref.refs_4_.refs_6_ = bf16[768,384]{1,0:T(8,128)(2,1)S(1)} collective-permute-done((bf16[768,384]{1,0:T(8,128)(2,1)}, bf16[768,384]{1,0:T(8,128)(2,1)S(1)}, u32[]{:S(2)}, u32[]{:S(2)}) %collective-permute-start.1) | collective-permute-done | bytes 589856 | tf_op jit(solution)/shard_map/ppermute | solution.py:58
  34.3 37.2 %collective-permute-done.2.refs_4_.refs_5_.refs_7_ = bf16[768,384]{1,0:T(8,128)(2,1)} collective-permute-done((bf16[768,384]{1,0:T(8,128)(2,1)S(1)}, bf16[768,384]{1,0:T(8,128)(2,1)}, u32[]{:S(2)}, u32[]{:S(2)}) %collective-permute-start.2) | collective-permute-done | bytes 589856 | tf_op jit(solution)/shard_map/ppermute | solution.py:58
  75.0 4.3 %collective-permute-done = bf16[1,8,384]{2,1,0:T(8,128)(2,1)S(1)} collective-permute-done((bf16[1,8,384]{2,1,0:T(8,128)(2,1)S(1)}, bf16[1,8,384]{2,1,0:T(8,128)(2,1)S(1)}, u32[]{:S(2)}, u32[]{:S(2)}) %collective-permute-start) | collective-permute-done | bytes 6176 | tf_op jit(solution)/shard_map/ppermute | solution.py:58
  82.7 5.2 %pad_frames.1 = (bf16[1664,768]{1,0:T(8,128)(2,1)}, bf16[1664,768]{1,0:T(8,128)(2,1)}) custom-call(bf16[4,392,768]{2,1,0:T(8,128)(2,1)} %x_ref.1, bf16[4,392,768]{2,1,0:T(8,128)(2,1)} %g_ref.1), custom_call_target="tpu_custom_call" | custom-call | flops 5500000256 | tf_op jit(solution)/shard_map/pad_frames/pallas_call | solution.py:538
  87.8 4.6 %copy.28 = bf16[1664,768]{0,1:T(8,128)(2,1)} copy(bf16[1664,768]{1,0:T(8,128)(2,1)} %get-tuple-element.29.refs_1_) | data formatting | bytes 5111808 | tf_op jit(solution)/shard_map/pad_frames/pallas_call | solution.py:538
  97.3 33.4 %attend.1 = (bf16[1664,768]{1,0:T(8,128)(2,1)}, bf16[1664,2304]{1,0:T(8,128)(2,1)}, bf16[1664,768]{1,0:T(8,128)(2,1)}, f32[1664,128]{1,0:T(8,128)}, f32[1664,768]{1,0:T(8,128)}, /*index=5*/bf16[1664,768]{1,0:T(8,128)(2,1)}) custom-call(bf16[1664,768]{1,0:T(8,128)(2,1)} %get-tuple-element.27.refs_0_, f32[8,768]{1,0:T(8,128)} %maximum_convert_fusion.refs_1_.refs_5_.refs_4_, ...), custom_call_target="tpu_custom_call" | custom-call | flops 32999999488 | tf_op jit(solution)/shard_map/attend/pallas_call | solution.py:549
  130.7 4.5 %copy.27 = bf16[1664,768]{0,1:T(8,128)(2,1)} copy(bf16[1664,768]{1,0:T(8,128)(2,1)} %get-tuple-element.28.refs_0_) | data formatting | bytes 5111808 | tf_op jit(solution)/shard_map/attend/pallas_call | solution.py:549
  136.2 71.3 %feed_forward.1 = (bf16[4,392,768]{2,1,0:T(8,128)(2,1)}, f32[1664,768]{1,0:T(8,128)}, f32[2,2,768,768]{3,2,1,0:T(8,128)}, bf16[2,2,768,768]{3,2,1,0:T(8,128)(2,1)}, f32[8,768]{1,0:T(8,128)}) custom-call(bf16[1664,768]{1,0:T(8,128)(2,1)} %get-tuple-element.28.refs_0_, bf16[1664,768]{1,0:T(8,128)(2,1)} %get-tuple-element.29.refs_1_, ...), custom_call_target="tpu_custom_call" | custom-call | flops 68200001536 | tf_op jit(solution)/shard_map/feed_forward/pallas_call | solution.py:587
  207.5 5.6 %fusion = f32[768,768]{1,0:T(8,128)S(1)} fusion(bf16[1664,768]{1,0:T(8,128)(2,1)} %get-tuple-element.37, f32[1664,768]{1,0:T(8,128)} %get-tuple-element.32.refs_0_.refs_1_), kind=kOutput, calls=%fused_computation.7 | convolution fusion | flops 1964212224 | bytes 10027008 | tf_op jit(solution)/shard_map/dot_general | solution.py:37
  213.8 25.9 %shard_map.212.refs_3_ = bf16[1664,1152]{1,0:T(8,128)(2,1)} custom-call(f32[1664,768]{1,0:T(8,128)} %get-tuple-element.32.refs_0_.refs_1_, bf16[1664,2304]{1,0:T(8,128)(2,1)} %get-tuple-element.33.refs_1_, f32[1664,128]{1,0:T(8,128)} %get-tuple-element.34.refs_2_, bf16[768,384]{1,0:T(8,128)(2,1)} %pack_near.1.refs_2_.refs_3_.refs_5_, ...), custom_call_target="tpu_custom_call" | custom-call | flops 27499999232 | tf_op jit(solution)/shard_map/pallas_call | solution.py:636
  239.8 6.3 %convolution_convert_fusion = bf16[1152,768]{1,0:T(8,128)(2,1)S(1)} fusion(bf16[1664,1152]{1,0:T(8,128)(2,1)} %shard_map.212.refs_3_, bf16[1664,768]{1,0:T(8,128)(2,1)} %get-tuple-element.36), kind=kOutput, calls=%fused_computation.2 | convolution fusion | flops 2945286144 | bytes 8159232 | tf_op jit(solution)/shard_map/dot_general | solution.py:37
  247.8 25.7 %shard_map.211.refs_2_ = bf16[1664,1152]{1,0:T(8,128)(2,1)} custom-call(f32[1664,768]{1,0:T(8,128)} %get-tuple-element.32.refs_0_.refs_1_, bf16[1664,2304]{1,0:T(8,128)(2,1)} %get-tuple-element.33.refs_1_, f32[1664,128]{1,0:T(8,128)} %get-tuple-element.34.refs_2_, bf16[768,384]{1,0:T(8,128)(2,1)} %pack_near.1.refs_2_.refs_3_.refs_5_, ...), custom_call_target="tpu_custom_call" | custom-call | flops 27499999232 | tf_op jit(solution)/shard_map/pallas_call | solution.py:636
  273.5 5.8 %fusion.27 = f32[1152,768]{1,0:T(8,128)S(1)} fusion(bf16[1664,1152]{1,0:T(8,128)(2,1)} %shard_map.211.refs_2_, bf16[1664,768]{1,0:T(8,128)(2,1)S(1)} %copy-done.26), kind=kOutput, calls=%fused_computation.79 | convolution fusion | flops 2944401408 | bytes 9928704 | tf_op jit(solution)/shard_map/dot_general | solution.py:37
  291.5 15.8 %input_gradient.1 = (f32[4,392,768]{2,1,0:T(8,128)}, f32[8,768]{1,0:T(8,128)}) custom-call(bf16[1664,768]{1,0:T(8,128)(2,1)} %get-tuple-element.27.refs_0_, f32[1664,768]{1,0:T(8,128)} %get-tuple-element.32.refs_0_.refs_1_, bf16[1664,1152]{1,0:T(8,128)(2,1)} %shard_map.211.refs_2_, bf16[1664,1152]{1,0:T(8,128)(2,1)} %shard_map.212.refs_3_, ...), custom_call_target="tpu_custom_call" | custom-call | flops 15399999488 | tf_op jit(solution)/shard_map/input_gradient/pallas_call | solution.py:676
  310.3 14.0 %collective-permute-done.25 = f32[8,768]{1,0:T(8,128)S(1)} collective-permute-done((f32[8,768]{1,0:T(8,128)S(1)}, f32[8,768]{1,0:T(8,128)S(1)}, u32[]{:S(2)}, u32[]{:S(2)}) %collective-permute-start.25) | collective-permute-done | bytes 24608 | tf_op jit(solution)/shard_map/ppermute | solution.py:58
  325.5 3.6 collective-permute-done.26
  339.5 6.7 %collective-permute-done.22 = bf16[2,2,192,384]{3,2,1,0:T(8,128)(2,1)S(1)} collective-permute-done((bf16[2,2,192,384]{3,2,1,0:T(8,128)(2,1)S(1)}, bf16[2,2,192,384]{3,2,1,0:T(8,128)(2,1)S(1)}, u32[]{:S(2)}, u32[]{:S(2)}) %collective-permute-start.22) | collective-permute-done | bytes 589856 | tf_op jit(solution)/shard_map/ppermute | solution.py:58
  347.5 3.4 collective-permute-done.34
  350.9 7.9 %collective-permute-done.32 = bf16[1,384,768]{2,1,0:T(8,128)(2,1)S(1)} collective-permute-done((bf16[1,384,768]{2,1,0:T(8,128)(2,1)S(1)}, bf16[1,384,768]{2,1,0:T(8,128)(2,1)S(1)}, u32[]{:S(2)}, u32[]{:S(2)}) %collective-permute-start.32) | collective-permute-done | bytes 589856 | tf_op jit(solution)/shard_map/ppermute | solution.py:58
  365.8 14.8 %collective-permute-done.35 = bf16[384,768]{1,0:T(8,128)(2,1)S(1)} collective-permute-done((bf16[384,768]{1,0:T(8,128)(2,1)}, bf16[384,768]{1,0:T(8,128)(2,1)S(1)}, u32[]{:S(2)}, u32[]{:S(2)}) %collective-permute-start.35) | collective-permute-done | bytes 589856 | tf_op jit(solution)/shard_map/ppermute | solution.py:58
  387.0 23.0 %collective-permute-done.28 = bf16[392,384]{1,0:T(8,128)(2,1)S(1)} collective-permute-done((bf16[392,384]{1,0:T(8,128)(2,1)S(1)}, bf16[392,384]{1,0:T(8,128)(2,1)S(1)}, u32[]{:S(2)}, u32[]{:S(2)}) %collective-permute-start.28) | collective-permute-done | bytes 301088 | tf_op jit(solution)/shard_map/ppermute | solution.py:58
  414.4 7.0 %collective-permute-done.29 = bf16[392,384]{1,0:T(8,128)(2,1)} collective-permute-done((bf16[392,384]{1,0:T(8,128)(2,1)}, bf16[392,384]{1,0:T(8,128)(2,1)}, u32[]{:S(2)}, u32[]{:S(2)}) %collective-permute-start.29) | collective-permute-done | bytes 301088 | tf_op jit(solution)/shard_map/ppermute | solution.py:58
  425.6 3.5 collective-permute-done.37
  (182 shorter events, 84.6 us)
Async XLA Ops:
  8.1 16.6 %collective-permute-start.1 = (bf16[768,384]{1,0:T(8,128)(2,1)}, bf16[768,384]{1,0:T(8,128)(2,1)S(1)}, u32[]{:S(2)}, u32[]{:S(2)}) collective-permute-start(bf16[768,384]{1,0:T(8,128)(2,1)} %pack_near.1.refs_2_.refs_3_.refs_5_), channel_id=1, source_target_pairs={{0,16},{16,0},{1,17},{17,1},{2,18},{18,2},{3,19},{19,3},{4,20},{20... | collective-permute-start | bytes 1769480 | tf_op jit(solution)/shard_map/ppermute | solution.py:58
  28.0 45.0 %collective-permute-start.10 = (bf16[1536,384]{1,0:T(8,128)(2,1)}, bf16[1536,384]{1,0:T(8,128)(2,1)S(1)}, u32[]{:S(2)}, u32[]{:S(2)}) collective-permute-start(bf16[1536,384]{1,0:T(8,128)(2,1)} %pack_feed.1.refs_6_), channel_id=1, source_target_pairs={{0,16},{16,0},{1,17},{17,1},{2,18},{18,2},{3,19},{19,3},{4,20},{20... | collective-permute-start | bytes 3538952 | tf_op jit(solution)/shard_map/ppermute | solution.py:58
  29.7 45.1 %collective-permute-start.11 = (bf16[1536,384]{1,0:T(8,128)(2,1)}, bf16[1536,384]{1,0:T(8,128)(2,1)S(1)}, u32[]{:S(2)}, u32[]{:S(2)}) collective-permute-start(bf16[1536,384]{1,0:T(8,128)(2,1)} %pack_feed.1.refs_6_), channel_id=1, source_target_pairs={{0,2},{1,3},{2,0},{3,1},{4,6},{5,7},{6,4},{7,5},{8,10},{9,11},{10,... | collective-permute-start | bytes 3538952 | tf_op jit(solution)/shard_map/ppermute | solution.py:58
  31.2 40.3 %collective-permute-start.2 = (bf16[768,384]{1,0:T(8,128)(2,1)S(1)}, bf16[768,384]{1,0:T(8,128)(2,1)}, u32[]{:S(2)}, u32[]{:S(2)}) collective-permute-start(bf16[768,384]{1,0:T(8,128)(2,1)S(1)} %copy-done.11), channel_id=1, source_target_pairs={{0,2},{1,3},{2,0},{3,1},{4,6},{5,7},{6,4},{7,5},{8,10},{9,11},{10,... | collective-permute-start | bytes 1769480 | tf_op jit(solution)/shard_map/ppermute | solution.py:58
  31.7 48.1 %collective-permute-start.5 = (bf16[768,384]{1,0:T(8,128)(2,1)S(1)}, bf16[768,384]{1,0:T(8,128)(2,1)S(1)}, u32[]{:S(2)}, u32[]{:S(2)}) collective-permute-start(bf16[768,384]{1,0:T(8,128)(2,1)S(1)} %copy-done.11), channel_id=1, source_target_pairs={{0,1},{1,0},{2,3},{3,2},{4,5},{5,4},{6,7},{7,6},{8,9},{9,8},{10,11... | collective-permute-start | bytes 1769480 | tf_op jit(solution)/shard_map/ppermute | solution.py:58
  32.7 46.6 %collective-permute-start.3 = (bf16[384,384]{1,0:T(8,128)(2,1)S(1)}, bf16[384,384]{1,0:T(8,128)(2,1)}, u32[]{:S(2)}, u32[]{:S(2)}) collective-permute-start(bf16[384,384]{1,0:T(8,128)(2,1)S(1)} %slice.138), channel_id=1, source_target_pairs={{0,2},{1,3},{2,0},{3,1},{4,6},{5,7},{6,4},{7,5},{8,10},{9,11},{10,... | collective-permute-start | bytes 884744 | tf_op jit(solution)/shard_map/ppermute | solution.py:58
  74.9 19.5 %collective-permute-start.6 = (bf16[768,384]{1,0:T(8,128)(2,1)S(1)}, bf16[768,384]{1,0:T(8,128)(2,1)}, u32[]{:S(2)}, u32[]{:S(2)}) collective-permute-start(bf16[768,384]{1,0:T(8,128)(2,1)S(1)} %copy-done.9), channel_id=1, source_target_pairs={{0,1},{1,0},{2,3},{3,2},{4,5},{5,4},{6,7},{7,6},{8,9},{9,8},{10,11... | collective-permute-start | bytes 1769480 | tf_op jit(solution)/shard_map/ppermute | solution.py:58
  94.3 40.9 %collective-permute-start.14 = (bf16[1536,384]{1,0:T(8,128)(2,1)S(1)}, bf16[1536,384]{1,0:T(8,128)(2,1)}, u32[]{:S(2)}, u32[]{:S(2)}) collective-permute-start(bf16[1536,384]{1,0:T(8,128)(2,1)S(1)} %copy-done.10), channel_id=1, source_target_pairs={{0,1},{1,0},{2,3},{3,2},{4,5},{5,4},{6,7},{7,6},{8,9},{9,8},{10,11... | collective-permute-start | bytes 3538952 | tf_op jit(solution)/shard_map/ppermute | solution.py:58
  94.4 40.8 %collective-permute-start.15 = (bf16[1536,384]{1,0:T(8,128)(2,1)}, bf16[1536,384]{1,0:T(8,128)(2,1)}, u32[]{:S(2)}, u32[]{:S(2)}) collective-permute-start(bf16[1536,384]{1,0:T(8,128)(2,1)} %copy-done.12), channel_id=1, source_target_pairs={{0,1},{1,0},{2,3},{3,2},{4,5},{5,4},{6,7},{7,6},{8,9},{9,8},{10,11... | collective-permute-start | bytes 3538952 | tf_op jit(solution)/shard_map/ppermute | solution.py:58
  94.8 40.4 %collective-permute-start.16 = (bf16[1536,384]{1,0:T(8,128)(2,1)}, bf16[1536,384]{1,0:T(8,128)(2,1)}, u32[]{:S(2)}, u32[]{:S(2)}) collective-permute-start(bf16[1536,384]{1,0:T(8,128)(2,1)} %copy-done.13), channel_id=1, source_target_pairs={{0,1},{1,0},{2,3},{3,2},{4,5},{5,4},{6,7},{7,6},{8,9},{9,8},{10,11... | collective-permute-start | bytes 3538952 | tf_op jit(solution)/shard_map/ppermute | solution.py:58
  95.2 40.0 %collective-permute-start.17 = (bf16[768,384]{1,0:T(8,128)(2,1)S(1)}, bf16[768,384]{1,0:T(8,128)(2,1)S(1)}, u32[]{:S(2)}, u32[]{:S(2)}) collective-permute-start(bf16[768,384]{1,0:T(8,128)(2,1)S(1)} %collective-permute-done.12.refs_9_), channel_id=1, source_target_pairs={{0,1},{1,0},{2,3},{3,2},{4,5},{5,4},{6,7},{7,6},{8,9},{9,8},{10,11... | collective-permute-start | bytes 1769480 | tf_op jit(solution)/shard_map/ppermute | solution.py:58
  97.3 37.9 %collective-permute-start.18 = (bf16[768,384]{1,0:T(8,128)(2,1)}, bf16[768,384]{1,0:T(8,128)(2,1)S(1)}, u32[]{:S(2)}, u32[]{:S(2)}) collective-permute-start(bf16[768,384]{1,0:T(8,128)(2,1)} %collective-permute-done.13.refs_10_), channel_id=1, source_target_pairs={{0,1},{1,0},{2,3},{3,2},{4,5},{5,4},{6,7},{7,6},{8,9},{9,8},{10,11... | collective-permute-start | bytes 1769480 | tf_op jit(solution)/shard_map/ppermute | solution.py:58
  213.3 70.3 %collective-permute-start.30 = (bf16[2,2,768,768]{3,2,1,0:T(8,128)(2,1)}, bf16[2,2,768,768]{3,2,1,0:T(8,128)(2,1)}, u32[]{:S(2)}, u32[]{:S(2)}) collective-permute-start(bf16[2,2,768,768]{3,2,1,0:T(8,128)(2,1)} %get-tuple-element.41), channel_id=1, source_target_pairs={{0,1},{1,0},{2,3},{3,2},{4,5},{5,4},{6,7},{7,6},{8,9},{9,8},{10,11... | collective-permute-start | bytes 14155784 | tf_op jit(solution)/shard_map/ppermute | solution.py:58
  247.7 31.7 %collective-permute-start.19 = (bf16[1536,768]{1,0:T(8,128)(2,1)}, bf16[1536,768]{1,0:T(8,128)(2,1)}, u32[]{:S(2)}, u32[]{:S(2)}) collective-permute-start(bf16[1536,768]{1,0:T(8,128)(2,1)} %pad_maximum_fusion), channel_id=1, source_target_pairs={{0,1},{1,0},{2,3},{3,2},{4,5},{5,4},{6,7},{7,6},{8,9},{9,8},{10,11... | collective-permute-start | bytes 7077896 | tf_op jit(solution)/shard_map/ppermute | solution.py:58
  282.6 48.0 %collective-permute-start.20 = (bf16[2,1,192,768]{3,2,1,0:T(8,128)(2,1)}, bf16[2,1,192,768]{3,2,1,0:T(8,128)(2,1)}, u32[]{:S(2)}, u32[]{:S(2)}) collective-permute-start(bf16[2,1,192,768]{3,2,1,0:T(8,128)(2,1)} %slice.199), channel_id=1, source_target_pairs={{0,2},{1,3},{2,0},{3,1},{4,6},{5,7},{6,4},{7,5},{8,10},{9,11},{10,... | collective-permute-start | bytes 1769480 | tf_op jit(solution)/shard_map/ppermute | solution.py:58
  286.7 45.4 %collective-permute-start.33 = (bf16[2,384,768]{2,1,0:T(8,128)(2,1)S(1)}, bf16[2,384,768]{2,1,0:T(8,128)(2,1)}, u32[]{:S(2)}, u32[]{:S(2)}) collective-permute-start(bf16[2,384,768]{2,1,0:T(8,128)(2,1)S(1)} %fusion.3), channel_id=1, source_target_pairs={{0,16},{16,0},{1,17},{17,1},{2,18},{18,2},{3,19},{19,3},{4,20},{20... | collective-permute-start | bytes 3538952 | tf_op jit(solution)/shard_map/ppermute | solution.py:58
  290.5 45.2 %collective-permute-start.31 = (bf16[1,768,768]{2,1,0:T(8,128)(2,1)}, bf16[1,768,768]{2,1,0:T(8,128)(2,1)}, u32[]{:S(2)}, u32[]{:S(2)}) collective-permute-start(bf16[1,768,768]{2,1,0:T(8,128)(2,1)} %fusion.4), channel_id=1, source_target_pairs={{0,2},{1,3},{2,0},{3,1},{4,6},{5,7},{6,4},{7,5},{8,10},{9,11},{10,... | collective-permute-start | bytes 3538952 | tf_op jit(solution)/shard_map/ppermute | solution.py:58
  337.3 21.5 %collective-permute-start.32 = (bf16[1,384,768]{2,1,0:T(8,128)(2,1)S(1)}, bf16[1,384,768]{2,1,0:T(8,128)(2,1)S(1)}, u32[]{:S(2)}, u32[]{:S(2)}) collective-permute-start(bf16[1,384,768]{2,1,0:T(8,128)(2,1)S(1)} %dynamic-slice_convert_fusion.1), channel_id=1, source_target_pairs={{0,16},{16,0},{1,17},{17,1},{2,18},{18,2},{3,19},{19,3},{4,20},{20... | collective-permute-start | bytes 1769480 | tf_op jit(solution)/shard_map/ppermute | solution.py:58
  338.9 23.9 %collective-permute-start.21 = (bf16[2,1,192,384]{3,2,1,0:T(8,128)(2,1)S(1)}, bf16[2,1,192,384]{3,2,1,0:T(8,128)(2,1)S(1)}, u32[]{:S(2)}, u32[]{:S(2)}) collective-permute-start(bf16[2,1,192,384]{3,2,1,0:T(8,128)(2,1)S(1)} %dynamic-slice_convert_fusion.4), channel_id=1, source_target_pairs={{0,16},{16,0},{1,17},{17,1},{2,18},{18,2},{3,19},{19,3},{4,20},{20... | collective-permute-start | bytes 884744 | tf_op jit(solution)/shard_map/ppermute | solution.py:58
  360.2 20.5 %collective-permute-start.35 = (bf16[384,768]{1,0:T(8,128)(2,1)}, bf16[384,768]{1,0:T(8,128)(2,1)S(1)}, u32[]{:S(2)}, u32[]{:S(2)}) collective-permute-start(bf16[384,768]{1,0:T(8,128)(2,1)} %fusion.6), channel_id=1, source_target_pairs={{0,4},{4,0},{8,12},{12,8},{1,5},{5,1},{9,13},{13,9},{2,6},{6,2},{1... | collective-permute-start | bytes 1769480 | tf_op jit(solution)/shard_map/ppermute | solution.py:58
  364.2 21.2 %collective-permute-start.27 = (bf16[392,384]{1,0:T(8,128)(2,1)S(1)}, bf16[392,384]{1,0:T(8,128)(2,1)S(1)}, u32[]{:S(2)}, u32[]{:S(2)}) collective-permute-start(bf16[392,384]{1,0:T(8,128)(2,1)S(1)} %dynamic-slice_convert_fusion.3), channel_id=1, source_target_pairs={{0,4},{4,0},{8,12},{12,8},{1,5},{5,1},{9,13},{13,9},{2,6},{6,2},{1... | collective-permute-start | bytes 903176 | tf_op jit(solution)/shard_map/ppermute | solution.py:58
  381.0 30.0 %collective-permute-start.36 = (bf16[384,768]{1,0:T(8,128)(2,1)S(1)}, bf16[384,768]{1,0:T(8,128)(2,1)S(1)}, u32[]{:S(2)}, u32[]{:S(2)}) collective-permute-start(bf16[384,768]{1,0:T(8,128)(2,1)S(1)} %fusion.23), channel_id=1, source_target_pairs={{0,8},{4,12},{8,0},{12,4},{1,9},{5,13},{9,1},{13,5},{2,10},{6,14},... | collective-permute-start | bytes 1769480 | tf_op jit(solution)/shard_map/ppermute | solution.py:58
  385.5 24.5 %collective-permute-start.28 = (bf16[392,384]{1,0:T(8,128)(2,1)S(1)}, bf16[392,384]{1,0:T(8,128)(2,1)S(1)}, u32[]{:S(2)}, u32[]{:S(2)}) collective-permute-start(bf16[392,384]{1,0:T(8,128)(2,1)S(1)} %fusion.10), channel_id=1, source_target_pairs={{0,8},{4,12},{8,0},{12,4},{1,9},{5,13},{9,1},{13,5},{2,10},{6,14},... | collective-permute-start | bytes 903176 | tf_op jit(solution)/shard_map/ppermute | solution.py:58
  412.4 16.6 %collective-permute-start.37 = (bf16[384,768]{1,0:T(8,128)(2,1)}, bf16[384,768]{1,0:T(8,128)(2,1)S(1)}, u32[]{:S(2)}, u32[]{:S(2)}) collective-permute-start(bf16[384,768]{1,0:T(8,128)(2,1)} %get-tuple-element.58), channel_id=1, source_target_pairs={{0,4},{4,0},{8,12},{12,8},{1,5},{5,1},{9,13},{13,9},{2,6},{6,2},{1... | collective-permute-start | bytes 1769480 | tf_op jit(solution)/shard_map/ppermute | solution.py:58
  (44 other events, 701.4 us)
where the time goes:
time: 439 us; the launch traced here: 432 us
  Pallas kernels  182 us (41%)
  waiting for transfers between devices  146 us (33%)
  starting transfers between devices  32.4 us (7%)
  local copies, waits for them, and re-layouts  29 us (7%)
  other arithmetic  23.1 us (5%)
  matrix products  17.8 us (4%)
    ppermute x38, waiting for transfers between devices, swap(): return lax.ppermute(block, axis, [(i, i ^ mask) for i in range(count)])  146 us
    pallas_call x1, Pallas kernels, on_device(): pl.pallas_call(functools.partial(forward_kernel, block_rows, feed, hidden...  71.3 us
    pallas_call x2, Pallas kernels, attention_back(): pl.pallas_call(functools.partial(backward_kernel, HEADS, head_size, side,...  51.6 us
    pallas_call x1, Pallas kernels, on_device(): pl.pallas_call(functools.partial(attend_kernel, HEADS, head_size, attenti...  33.4 us
    ppermute x38, starting transfers between devices, swap(): return lax.ppermute(block, axis, [(i, i ^ mask) for i in range(count)])  32.4 us
    dot_general x3, matrix products, dot_left_t(): lax.dot_general(left, right, (((0,), (0,)), ((), ())), preferred_element_...  17.8 us
    pallas_call x1, Pallas kernels, on_device(): pl.pallas_call(functools.partial(input_kernel, attention, units), name='i...  15.8 us
    unnamed x64, local copies, waits for them, and re-layouts  11.7 us
  transfers between devices with their start and end apart: 38, of which 18 were waited for; matrix products, arithmetic and copies ran while one was open for 12% of the time, Pallas kernels for 25%

commit v1 on v0

v1 whole, which is shorter than its diff:
```python
import functools
import math

import jax
import jax.numpy as jnp
from jax import lax
from jax.experimental import pallas as pl
from jax.experimental.pallas import tpu as pltpu
from jax.sharding import PartitionSpec as P


HEADS = 12
PLACES = 196
PADDED = 208

EPSILON = 1e-06
INV_ROOT_TWO = 0.7071067811865476
INV_ROOT_TAU = 0.3989422804014327
LOWEST = -1e30

VMEM_BYTES = 60 * 1024 * 1024


def dot_rows(left, right):
    return lax.dot_general(
        left, right, (((1,), (0,)), ((), ())), preferred_element_type=jnp.float32
    )


def dot_right_t(left, right):
    return lax.dot_general(
        left, right, (((1,), (1,)), ((), ())), preferred_element_type=jnp.float32
    )


def dot_left_t(left, right):
    return lax.dot_general(
        left, right, (((0,), (0,)), ((), ())), preferred_element_type=jnp.float32
    )


def standardize_rows(rows_in):
    center = rows_in - jnp.mean(rows_in, axis=-1, keepdims=True)
    spread = jnp.mean(center * center, axis=-1, keepdims=True)
    reciprocal_spread = lax.rsqrt(spread + EPSILON)
    return (center * reciprocal_spread, reciprocal_spread)


def norm_backward_pass(norm_gradient, gain_vector, centered_rows, reciprocal_spread):
    scaled_result = norm_gradient * gain_vector
    leading_part = jnp.mean(scaled_result, axis=-1, keepdims=True)
    trailing_part = jnp.mean(scaled_result * centered_rows, axis=-1, keepdims=True)
    return reciprocal_spread * (scaled_result - leading_part - centered_rows * trailing_part)


def swap(block, axis, mask):
    count = lax.axis_size(axis)
    return lax.ppermute(block, axis, [(i, i ^ mask) for i in range(count)])


def bits_of(axis):
    return [(axis, 1 << b) for b in reversed(range(lax.axis_size(axis).bit_length() - 1))]


def orders():
    along_f, along_t = bits_of("fsdp"), bits_of("tp")
    first, last = along_t[:-1], along_t[-1:]
    return (along_f + first + last, first + along_f + last)


def piece_masks():
    masks = [0]
    for _, mask in bits_of("tp"):
        masks = [m for m in masks] + [m ^ mask for m in masks]
    return masks


class Pack:
    def __init__(self, arrays, pieces, part):
        self.arrays, self.pieces, self.part = arrays, pieces, part

    def copies(self, refs, piece, first, count, target, row):
        mine = lax.axis_index("fsdp")
        made = []
        for array, start, rows, place, mask in self.pieces[piece]:
            low, high = max(first, place), min(first + count, place + rows)
            if low >= high:
                continue
            source = refs[array].at[pl.ds(start + low - place, high - low), :]
            where = pl.ds(row + low - first, high - low)
            if mask is None:
                made.append((source, target.at[where, :]))
            else:
                column = pl.multiple_of((mine ^ mask) * self.part, 128)
                made.append((source, target.at[where, pl.ds(column, self.part)]))
        return made


def copies_on(pairs, sems, at=0):
    return [
        pltpu.make_async_copy(source, target, sems.at[at + n])
        for n, (source, target) in enumerate(pairs)
    ]


def start_all(copies):
    for copy in copies:
        copy.start()


def wait_all(copies):
    for copy in copies:
        copy.wait()


def gather_pack(block):
    f_count, t_count = lax.axis_size("fsdp"), lax.axis_size("tp")
    rows, part = block.shape
    if f_count == 2 and t_count == 4 and part % 128 == 0:
        half = rows // 2
        beside_f = swap(block, "fsdp", 1)
        beside_t = swap(block, "tp", 2)
        across = (swap(beside_f[:half], "tp", 2), swap(beside_t[half:], "fsdp", 1))
        here = (block, beside_f, beside_t) + across
        there = tuple(swap(array, "tp", 1) for array in here)
        pieces = []
        for base in (0, len(here)):
            pieces.append([(base, 0, rows, 0, 0), (base + 1, 0, rows, 0, 1)])
            pieces.append(
                [
                    (base + 2, 0, rows, 0, 0),
                    (base + 3, 0, half, 0, 1),
                    (base + 4, 0, half, half, 1),
                ]
            )
        return Pack(here + there, pieces, part)
    held, keys = block[None], [(0, 0)]
    for axis, mask in orders()[0]:
        held = jnp.concatenate([held, swap(held, axis, mask)], axis=0)
        keys = keys + [(f ^ mask, t) if axis == "fsdp" else (f, t ^ mask) for f, t in keys]
    place = {key: n for n, key in enumerate(keys)}
    mine = lax.axis_index("fsdp")
    full = []
    for t in piece_masks():
        stacked = jnp.stack([held[place[(f, t)]] for f in range(f_count)])
        parts = [
            lax.dynamic_index_in_dim(stacked, mine ^ f, 0, keepdims=False)
            for f in range(f_count)
        ]
        full.append(jnp.concatenate(parts, axis=1))
    pieces = [[(p, 0, rows, 0, None)] for p in range(t_count)]
    return Pack(tuple(full), pieces, part)


def gather_columns(vectors):
    held, masks = [jnp.concatenate(vectors)], [0]
    for axis, mask in bits_of("fsdp"):
        got = swap(jnp.concatenate(held), axis, mask)
        held = held + jnp.split(got, len(held))
        masks = masks + [m ^ mask for m in masks]
    mine = lax.axis_index("fsdp")
    count = len(held)
    parts = [held[masks.index(m)].reshape(len(vectors), -1) for m in range(count)]
    if count == 2:
        first = mine == 0
        parts = [jnp.where(first, parts[0], parts[1]), jnp.where(first, parts[1], parts[0])]
    else:
        stacked = jnp.stack(parts)
        parts = [
            lax.dynamic_index_in_dim(stacked, mine ^ m, 0, keepdims=False) for m in range(count)
        ]
    return jnp.pad(jnp.concatenate(parts, axis=1), ((0, 8 - len(vectors)), (0, 0)))


def reduce_step(held, step, piece_axis, part_axis):
    axis, mask = step
    if axis == "tp":
        half = held.shape[piece_axis] // 2
        keep = lax.slice_in_dim(held, 0, half, axis=piece_axis)
        sent = lax.slice_in_dim(held, half, 2 * half, axis=piece_axis)
    else:
        part = held.shape[part_axis] // 2
        bit = jnp.where((lax.axis_index("fsdp") & mask) != 0, 1, 0)
        keep = lax.dynamic_slice_in_dim(held, bit * part, part, part_axis)
        sent = lax.dynamic_slice_in_dim(held, (1 - bit) * part, part, part_axis)
    return keep + swap(sent.astype(jnp.bfloat16), axis, mask).astype(jnp.float32)


def sum_over_ctx(block):
    count = lax.axis_size("ctx")
    bit = lax.axis_index("ctx") & 1
    rows = block.shape[0] // 2
    sent = lax.dynamic_slice_in_dim(block, (1 - bit) * rows, rows, 0)
    got = swap(sent.astype(jnp.bfloat16), "ctx", 1)
    held = lax.dynamic_slice_in_dim(block, bit * rows, rows, 0) + got.astype(jnp.float32)
    mask = 2
    while mask < count:
        got = swap(held.astype(jnp.bfloat16), "ctx", mask)
        held = held + got.astype(jnp.float32)
        mask *= 2
    other = swap(held.astype(jnp.bfloat16), "ctx", 1).astype(jnp.float32)
    return jnp.where(
        bit == 0,
        jnp.concatenate([held, other], axis=0),
        jnp.concatenate([other, held], axis=0),
    )


def sum_over(block, axes):
    for axis in axes:
        for _, mask in reversed(bits_of(axis)):
            block = block + swap(block, axis, mask)
    return block


def params():
    return pltpu.CompilerParams(vmem_limit_bytes=VMEM_BYTES)


def cost(micros):
    return pl.CostEstimate(flops=int(micros * 1.1e9), bytes_accessed=0, transcendentals=0)


def whole(shape):
    return pl.BlockSpec(shape, lambda i: (0,) * len(shape), pipeline_mode=pl.Buffered(1))


def rows_of(count, width, column=0):
    return pl.BlockSpec((count, width), lambda i: (i, column))


def in_place(arrays):
    return [pl.BlockSpec(memory_space=pl.ANY)] * len(arrays)


def prepare_kernel(count, x_ref, g_ref, norm_ref, xo_ref, go_ref, got_ref, xn_ref):
    blank = jnp.zeros((PADDED - PLACES, x_ref.shape[2]), jnp.float32)
    block_rows = count * PADDED

    def padded(block):
        parts = []
        for n in range(count):
            parts += [block[n * PLACES : (n + 1) * PLACES], blank]
        return jnp.concatenate(parts, axis=0)

    def one_block(n, carry):
        rows = pl.ds(pl.multiple_of(n * block_rows, 16), block_rows)
        tokens = padded(x_ref[n].astype(jnp.float32))
        xo_ref[rows, :] = tokens.astype(jnp.bfloat16)
        hat, _ = standardize_rows(tokens)
        xn_ref[rows, :] = (hat * norm_ref[0:1, :] + norm_ref[1:2, :]).astype(jnp.bfloat16)
        go_ref[rows, :] = padded(g_ref[n].astype(jnp.float32)).astype(jnp.bfloat16)
        return carry

    lax.fori_loop(0, x_ref.shape[0], one_block, 0)
    turn(go_ref, got_ref)


def turn(source, target):
    for start in range(0, source.shape[0], 128):
        target[:, start : start + 128] = source[start : start + 128, :].T


def turn_kernel(source_ref, target_ref):
    turn(source_ref, target_ref)


def pack_near_kernel(q_ref, k_ref, v_ref, o_ref, out_ref):
    units = q_ref.shape[0]
    for n, ref in enumerate((q_ref, k_ref, v_ref, o_ref)):
        out_ref[n * units : (n + 1) * units, :] = ref[...]


def pack_feed_kernel(up_ref, down_ref, gate_ref, out_ref):
    units = up_ref.shape[1]
    out_ref[:units, :] = up_ref[...].T
    out_ref[units:, :] = down_ref[...]


def unpad(block):
    count = block.shape[0] // PADDED
    return jnp.concatenate(
        [block[n * PADDED : n * PADDED + PLACES] for n in range(count)], axis=0
    )


def low_lanes(head_size):
    lane = lax.broadcasted_iota(jnp.int32, (1, 2 * head_size), 1)
    return lane < head_size


def staggered(count, begin, middle, end):
    begun, half_done = {0: begin(0)}, {}
    for n in range(count + 1):
        if n + 1 < count:
            begun[n + 1] = begin(n + 1)
        if n < count:
            half_done[n] = middle(n, begun.pop(n))
        if n > 0:
            end(n - 1, half_done.pop(n - 1))


def both_hands(block, low_half):
    blank = jnp.zeros_like(block)
    return jnp.concatenate(
        [jnp.where(low_half, block, blank), jnp.where(low_half, blank, block)], axis=0
    )


def projection_copies(pack, refs, units, target, groups):
    pieces = len(pack.pieces)
    side = pieces // 2 * units
    made = []
    for group in groups:
        half, kind = divmod(group, 3)
        for n in range(pieces // 2):
            row = group * side + n * units
            made += pack.copies(
                refs, half * pieces // 2 + n, kind * units, units, target, row
            )
    return made


def attend_kernel(heads, head_size, pack, units, *refs):
    count = len(pack.arrays)
    x_ref, xn_ref, norm_ref = refs[:3]
    raw = refs[3 : 3 + count]
    qkv_ref, mixed_ref, log_ref, hidden_ref, sn_ref = refs[3 + count : 8 + count]
    wqkv_ref, wout_ref, sems = refs[8 + count :]
    width = heads * head_size
    side = width // 2

    first = pl.program_id(0) == 0
    batches, used = [], 0
    for n in range(3):
        pairs = projection_copies(pack, raw, units, wqkv_ref, (2 * n, 2 * n + 1))
        batches.append(copies_on(pairs, sems, used))
        used += len(pairs)
    pairs = []
    for p in range(len(pack.pieces)):
        pairs += pack.copies(raw, p, 3 * units, units, wout_ref, p * units)
    batches.append(copies_on(pairs, sems, used))

    @pl.when(first)
    def _():
        for batch in batches:
            start_all(batch)

    normed = xn_ref[...]

    def project(n, carry):
        for k in range(3):

            @pl.when(first & (n == k))
            def _(k=k):
                wait_all(batches[k])

        cut = pl.ds(pl.multiple_of(n * width, 128), width)
        qkv_ref[:, cut] = dot_right_t(normed, wqkv_ref[cut, :]).astype(jnp.bfloat16)
        return carry

    lax.fori_loop(0, 3, project, 0)
    low_half = low_lanes(head_size)
    scale = 1.0 / math.sqrt(head_size)

    def one_frame(n, carry):
        rows = pl.ds(pl.multiple_of(n * PADDED, 16), PADDED)
        valid = lax.broadcasted_iota(jnp.int32, (1, PADDED), 1) < PLACES

        def begin(pair):
            half, place = divmod(pair, heads // 4)
            at = 3 * half * side + place * 2 * head_size
            q2 = qkv_ref[rows, at : at + 2 * head_size] * jnp.bfloat16(scale)
            k2 = qkv_ref[rows, side + at : side + at + 2 * head_size]
            return dot_right_t(both_hands(q2, low_half), k2)

        def middle(pair, scores):
            scores = jnp.where(valid, scores, LOWEST)
            top = jnp.max(scores, axis=-1, keepdims=True)
            powers = jnp.exp(scores - top)
            total = jnp.sum(powers, axis=-1, keepdims=True)
            logs = top + jnp.log(total)
            log_ref[rows, 2 * pair : 2 * pair + 1] = logs[:PADDED]
            log_ref[rows, 2 * pair + 1 : 2 * pair + 2] = logs[PADDED:]
            return (powers * (1.0 / total)).astype(jnp.bfloat16)

        def end(pair, probs):
            half, place = divmod(pair, heads // 4)
            at = (3 * half + 2) * side + place * 2 * head_size
            outs = dot_rows(probs, qkv_ref[rows, at : at + 2 * head_size])
            mixed_ref[rows, 2 * pair * head_size : 2 * (pair + 1) * head_size] = jnp.where(
                low_half, outs[:PADDED], outs[PADDED:]
            ).astype(jnp.bfloat16)

        staggered(heads // 2, begin, middle, end)
        return carry

    lax.fori_loop(0, normed.shape[0] // PADDED, one_frame, 0)

    @pl.when(first)
    def _():
        wait_all(batches[3])

    hidden = x_ref[...].astype(jnp.float32) + dot_rows(mixed_ref[...], wout_ref[...])
    hidden_ref[...] = hidden
    hat2, _ = standardize_rows(hidden)
    sn_ref[...] = (hat2 * norm_ref[2:3, :] + norm_ref[3:4, :]).astype(jnp.bfloat16)


def forward_kernel(tile, pack, units, *refs):
    count = len(pack.arrays)
    arrays, norm_ref = refs[:5], refs[5]
    raw = refs[6 : 6 + count]
    out_any, low_any, keep_any, send_ref, ngrad_ref = refs[6 + count : 11 + count]
    held = refs[11 + count : 16 + count]
    sn_ref, cot_ref, snt_ref, cott_ref, hidden_ref = held
    (
        y_ref, dh_ref, act_ref, din_ref, next_ref, wup_ref, wdown_ref, wupt_ref, wdownt_ref,
        keep_ref, out_ref, low_ref, sems, held_sems, keep_sems, out_sems, low_sems,
    ) = refs[16 + count :]
    step, steps = pl.program_id(0), len(pack.pieces)
    tiles = sn_ref.shape[0] // tile
    chunk = sn_ref.shape[1] // tiles
    wide = 2 * tile
    order = [(n + steps // 2) % steps for n in range(steps)]
    late = copies_on(zip(arrays, held), held_sems)

    def copies_of(n):
        pairs = pack.copies(raw, order[n], 0, units, next_ref.at[0], 0)
        pairs += pack.copies(raw, order[n], units, units, next_ref.at[1], 0)
        return copies_on(pairs, sems)

    @pl.when(step == 0)
    def _():
        start_all(copies_of(0) + late)
        y_ref[...] = jnp.zeros_like(y_ref)
        dh_ref[...] = jnp.zeros_like(dh_ref)

    def settle(n, size):
        rows = pl.ds(pl.multiple_of(n * size, 128), size)
        for place, plain, turned in ((0, wup_ref, wupt_ref), (1, wdown_ref, wdownt_ref)):
            block = next_ref[place, rows, :]
            plain[rows, :] = block
            turned[:, rows] = block.T

    def settle_all():
        def one(n, carry):
            settle(n, units // 2)
            return carry

        lax.fori_loop(0, 2, one, 0)

    @pl.when(step == 0)
    def _():
        wait_all(copies_of(0))
        settle_all()
        start_all(copies_of(1))
        wait_all(late[:2])

    def one_tile(n, carry):
        rows = pl.ds(pl.multiple_of(n * wide, 16), wide)
        inner = dot_rows(sn_ref[rows, :], wupt_ref[...])
        d_active = dot_rows(cot_ref[rows, :], wdownt_ref[...])
        share = 0.5 * (1.0 + lax.erf(inner * INV_ROOT_TWO))
        active = (inner * share).astype(jnp.bfloat16)
        slope = share + inner * (jnp.exp(-0.5 * inner * inner) * INV_ROOT_TAU)
        d_inner = (d_active * slope).astype(jnp.bfloat16)
        act_ref[rows, :] = active
        din_ref[rows, :] = d_inner
        y_ref[rows, :] += dot_rows(active, wdown_ref[...])
        dh_ref[rows, :] += dot_rows(d_inner, wup_ref[...])
        return carry

    lax.fori_loop(0, tiles // 2, one_tile, 0)

    @pl.when(step == 0)
    def _():
        wait_all(late[2:4])

    def weight_gradients(rows):
        keep_ref[0, rows, :] = dot_rows(snt_ref[rows, :], din_ref[...])
        keep_ref[1, rows, :] = dot_rows(cott_ref[rows, :], act_ref[...])

    def whole_keep(p):
        return pltpu.make_async_copy(
            keep_ref, keep_any.at[p - steps // 2], keep_sems.at[0]
        )

    for p in range(steps // 2 + 1, steps):

        @pl.when(step == p)
        def _(p=p):
            whole_keep(p - 1).wait()

    for p in range(1, steps):

        @pl.when(step == p - 1)
        def _(p=p):
            wait_all(copies_of(p))

    @pl.when(step < steps - 1)
    def _():
        weight_gradients(slice(None))
        for n in range(2):
            settle(n, units // 2)

    @pl.when(step < steps // 2)
    def _():
        send_ref[0] = keep_ref[...].astype(jnp.bfloat16)

    for p in range(steps // 2, steps - 1):

        @pl.when(step == p)
        def _(p=p):
            whole_keep(p).start()

    for p in range(2, steps):

        @pl.when(step == p - 2)
        def _(p=p):
            start_all(copies_of(p))

    @pl.when(step == steps - 1)
    def _():
        ngrad_ref[...] = jnp.zeros_like(ngrad_ref)
        wait_all(late[4:])

        def results(n):
            rows = pl.ds(pl.multiple_of(n * tile, 16), tile)
            part = pl.ds(pl.multiple_of(n * chunk, 16), chunk)
            return [
                pltpu.make_async_copy(out_ref.at[n], out_any.at[n], out_sems.at[n]),
                pltpu.make_async_copy(low_ref.at[rows, :], low_any.at[rows, :], low_sems.at[n]),
                pltpu.make_async_copy(
                    keep_ref.at[:, part, :],
                    keep_any.at[steps // 2 - 1, :, part, :],
                    keep_sems.at[1 + n],
                ),
            ]

        def close(n, carry):
            weight_gradients(pl.ds(pl.multiple_of(n * chunk, 16), chunk))
            rows = pl.ds(pl.multiple_of(n * tile, 16), tile)
            hidden = hidden_ref[rows, :]
            out_ref[n] = unpad(hidden + y_ref[rows, :]).astype(jnp.bfloat16)
            hat2, scale2 = standardize_rows(hidden)
            d_second = dh_ref[rows, :]
            d_hidden = cot_ref[rows, :].astype(jnp.float32) + norm_backward_pass(
                d_second, norm_ref[2:3, :], hat2, scale2
            )
            low_ref[rows, :] = d_hidden.astype(jnp.bfloat16)
            ngrad_ref[2:3, :] += jnp.sum(d_second * hat2, axis=0, keepdims=True)
            ngrad_ref[3:4, :] += jnp.sum(d_second, axis=0, keepdims=True)
            start_all(results(n))
            return carry

        lax.fori_loop(0, tiles, close, 0)
        for n in range(tiles):
            wait_all(results(n))


def backward_kernel(heads, head_size, half, pack, units, *refs):
    count = len(pack.arrays)
    low_ref, qkv_ref, log_ref = refs[:3]
    raw = refs[3 : 3 + count]
    dqkv_ref, dmix_ref, wout_ref, sems = refs[-4:]
    side = heads // 2 * head_size
    scale = 1.0 / math.sqrt(head_size)
    here = len(pack.pieces) // 2

    @pl.when(pl.program_id(0) == 0)
    def _():
        pairs = []
        for n in range(here):
            pairs += pack.copies(raw, half * here + n, 3 * units, units, wout_ref, n * units)
        copies = copies_on(pairs, sems)
        start_all(copies)
        wait_all(copies)

    low = low_ref[...]
    dmix_ref[...] = dot_right_t(low, wout_ref[...]).astype(jnp.bfloat16)
    low_half = low_lanes(head_size)

    def one_frame(n, carry):
        rows = pl.ds(pl.multiple_of(n * PADDED, 16), PADDED)
        valid = lax.broadcasted_iota(jnp.int32, (1, PADDED), 1) < PLACES

        def part(kind, pair):
            at = kind * side + pair * 2 * head_size
            return slice(at, at + 2 * head_size)

        def begin(pair):
            qm = both_hands(qkv_ref[rows, part(0, pair)] * jnp.bfloat16(scale), low_half)
            gm = both_hands(dmix_ref[rows, part(0, pair)], low_half)
            scores = dot_right_t(qm, qkv_ref[rows, part(1, pair)])
            return qm, gm, scores, dot_right_t(gm, qkv_ref[rows, part(2, pair)])

        def middle(pair, begun):
            qm, gm, scores, d_probs = begun
            head = half * (heads // 2) + 2 * pair
            log_total = jnp.concatenate(
                [log_ref[rows, head : head + 1], log_ref[rows, head + 1 : head + 2]], axis=0
            )
            probs = jnp.exp(jnp.where(valid, scores, LOWEST) - log_total)
            delta = jnp.sum(d_probs * probs, axis=-1, keepdims=True)
            d_scores = (probs * (d_probs - delta)).astype(jnp.bfloat16)
            return qm, gm, probs.astype(jnp.bfloat16), d_scores

        def end(pair, half_done):
            qm, gm, probs_low, d_scores = half_done
            dq = dot_rows(d_scores, qkv_ref[rows, part(1, pair)])
            dq = jnp.where(low_half, dq[:PADDED], dq[PADDED:]) * scale
            dqkv_ref[rows, part(0, pair)] = dq.astype(jnp.bfloat16)
            dqkv_ref[rows, part(1, pair)] = dot_left_t(d_scores, qm).astype(jnp.bfloat16)
            dqkv_ref[rows, part(2, pair)] = dot_left_t(probs_low, gm).astype(jnp.bfloat16)

        staggered(heads // 4, begin, middle, end)
        return carry

    lax.fori_loop(0, low.shape[0] // PADDED, one_frame, 0)


def gradient_kernel(left_ref, right_ref, out_ref):
    out_ref[...] = dot_left_t(left_ref[...], right_ref[...])


def gradients_kernel(left_ref, right_ref, other_ref, *refs):
    out_ref = refs[-1]
    step = pl.program_id(0)

    def put(block):
        if len(refs) > 1:
            block = block + refs[0][...].astype(jnp.float32)
        out_ref[...] = block.astype(out_ref.dtype)

    @pl.when(step < 3)
    def _():
        put(dot_left_t(left_ref[...], right_ref[...]))

    @pl.when(step == 3)
    def _():
        put(other_ref[...])


def input_kernel(pack, units, *refs):
    count = len(pack.arrays)
    x_ref, low_ref, first_ref, last_ref, norm_ref = refs[:5]
    raw = refs[5 : 5 + count]
    grad_ref, ngrad_ref, wqkv_ref, sems = refs[5 + count :]
    side = first_ref.shape[1]

    first = pl.program_id(0) == 0
    copies = copies_on(projection_copies(pack, raw, units, wqkv_ref, range(6)), sems)

    @pl.when(first)
    def _():
        start_all(copies)
        ngrad_ref[...] = jnp.zeros_like(ngrad_ref)

    hat1, scale1 = standardize_rows(x_ref[...].astype(jnp.float32))

    @pl.when(first)
    def _():
        wait_all(copies)

    d_first = dot_rows(first_ref[...], wqkv_ref[:side, :])
    d_first += dot_rows(last_ref[...], wqkv_ref[side:, :])
    total = unpad(low_ref[...].astype(jnp.float32) + norm_backward_pass(d_first, norm_ref[0:1, :], hat1, scale1))
    for n in range(grad_ref.shape[0]):
        grad_ref[n] = total[n * grad_ref.shape[1] : (n + 1) * grad_ref.shape[1]]
    ngrad_ref[0:1, :] += jnp.sum(d_first * hat1, axis=0, keepdims=True)
    ngrad_ref[1:2, :] += jnp.sum(d_first, axis=0, keepdims=True)


def on_device(
    frames_in,
    out_grad,
    w_query,
    w_key,
    w_value,
    w_out,
    w_up,
    w_down,
    norm1_gain,
    norm1_bias,
    norm2_gain,
    norm2_bias,
):
    block_count, resident_rows, width = frames_in.shape
    frames_each = resident_rows // PLACES
    block_rows = frames_each * PADDED
    rows = block_count * block_rows
    two = 2 * block_rows
    head_size = width // HEADS
    units = w_query.shape[1]
    part = w_query.shape[0]
    hidden_units = w_up.shape[1]
    order_a, order_b = orders()
    pieces = lax.axis_size("tp")
    low, full = jnp.bfloat16, jnp.float32
    sds = jax.ShapeDtypeStruct

    near = pl.pallas_call(
        pack_near_kernel,
        name="pack_near",
        out_shape=sds((4 * units, part), low),
        compiler_params=params(),
    )(w_query.T, w_key.T, w_value.T, w_out)
    attention = gather_pack(near)
    norms = gather_columns([norm1_gain, norm1_bias, norm2_gain, norm2_bias]).astype(full)
    feed_here = pl.pallas_call(
        pack_feed_kernel,
        name="pack_feed",
        in_specs=[pl.BlockSpec(memory_space=pltpu.VMEM)] * 2
        + [pl.BlockSpec(memory_space=pl.ANY)],
        out_shape=sds((2 * hidden_units, part), low),
        compiler_params=params(),
    )(w_up, w_down, attention.arrays[1])
    feed = gather_pack(feed_here)

    resident_two = pl.BlockSpec((2, resident_rows, width), lambda i: (i, 0, 0))
    tokens, cotangent, cotangent_t, normed = pl.pallas_call(
        functools.partial(prepare_kernel, frames_each),
        name="prepare",
        out_shape=[
            sds((rows, width), low),
            sds((rows, width), low),
            sds((width, rows), low),
            sds((rows, width), low),
        ],
        compiler_params=params(),
        cost_estimate=cost(9),
    )(frames_in, out_grad, norms)

    qkv, mixed, logs, hidden, second = pl.pallas_call(
        functools.partial(attend_kernel, HEADS, head_size, attention, units),
        name="attend",
        grid=(block_count // 2,),
        in_specs=[rows_of(two, width), rows_of(two, width), whole((8, width))]
        + in_place(attention.arrays),
        out_specs=[
            rows_of(two, 3 * width),
            rows_of(two, width),
            rows_of(two, 128),
            rows_of(two, width),
            rows_of(two, width),
        ],
        out_shape=[
            sds((rows, 3 * width), low),
            sds((rows, width), low),
            sds((rows, 128), full),
            sds((rows, width), full),
            sds((rows, width), low),
        ],
        scratch_shapes=[
            pltpu.VMEM((3 * width, width), low),
            pltpu.VMEM((width, width), low),
            pltpu.SemaphoreType.DMA((64,)),
        ],
        compiler_params=params(),
        cost_estimate=cost(30),
    )(tokens, normed, norms, *attention.arrays)

    second_t = pl.pallas_call(
        turn_kernel,
        name="turn",
        out_shape=sds((width, rows), low),
        compiler_params=params(),
        cost_estimate=cost(5),
    )(second)

    half = pieces // 2
    send_block = pl.BlockSpec(
        (1, 2, width, hidden_units), lambda i: (jnp.minimum(i, half - 1), 0, 0, 0)
    )
    block_out, hidden_low, feed_keep, feed_send, second_terms = pl.pallas_call(
        functools.partial(forward_kernel, block_rows, feed, hidden_units),
        name="feed_forward",
        grid=(pieces,),
        in_specs=in_place((second, cotangent, second_t, cotangent_t, hidden))
        + [whole((8, width))]
        + in_place(feed.arrays),
        out_specs=in_place(("block_out", "hidden_low", "feed_keep"))
        + [send_block, whole((8, width))],
        out_shape=[
            sds(frames_in.shape, low),
            sds((rows, width), low),
            sds((half, 2, width, hidden_units), full),
            sds((half, 2, width, hidden_units), low),
            sds((8, width), full),
        ],
        scratch_shapes=[
            pltpu.VMEM((rows, width), low),
            pltpu.VMEM((rows, width), low),
            pltpu.VMEM((width, rows), low),
            pltpu.VMEM((width, rows), low),
            pltpu.VMEM((rows, width), full),
            pltpu.VMEM((rows, width), full),
            pltpu.VMEM((rows, width), full),
            pltpu.VMEM((rows, hidden_units), low),
            pltpu.VMEM((rows, hidden_units), low),
            pltpu.VMEM((2, hidden_units, width), low),
            pltpu.VMEM((hidden_units, width), low),
            pltpu.VMEM((hidden_units, width), low),
            pltpu.VMEM((width, hidden_units), low),
            pltpu.VMEM((width, hidden_units), low),
            pltpu.VMEM((2, width, hidden_units), full),
            pltpu.VMEM(frames_in.shape, low),
            pltpu.VMEM((rows, width), low),
            pltpu.SemaphoreType.DMA((16,)),
            pltpu.SemaphoreType.DMA((5,)),
            pltpu.SemaphoreType.DMA((1 + block_count,)),
            pltpu.SemaphoreType.DMA((block_count,)),
            pltpu.SemaphoreType.DMA((block_count,)),
        ],
        compiler_params=params(),
        cost_estimate=cost(62),
    )(second, cotangent, second_t, cotangent_t, hidden, norms, *feed.arrays)

    last = order_a[-1]
    steps_a, steps_b = order_a[:-1][::-1], order_b[:-1][::-1]
    feed_got = swap(feed_send, *last)
    side = width // 2
    out_total = pl.pallas_call(
        gradient_kernel,
        name="out_gradient",
        grid=(2,),
        in_specs=[pl.BlockSpec((rows, side), lambda i: (0, i)), whole((rows, width))],
        out_specs=rows_of(side, width),
        out_shape=sds((width, width), full),
        compiler_params=params(),
        cost_estimate=cost(4),
    )(mixed, hidden_low)
    up_held = feed_keep[:, 0] + feed_got[:, 0].astype(full)
    down_held = feed_keep[:, 1] + feed_got[:, 1].astype(full)

    wide = 3 * width // 2

    def attention_back(side, group, begun):
        each = block_count // 4
        base = group * each

        def at(count, columns, column=0):
            return pl.BlockSpec((count, columns), lambda i: (base + i, column))

        begun = () if begun is None else (begun,)
        operands = (hidden_low, qkv, logs) + attention.arrays + begun
        return pl.pallas_call(
            functools.partial(backward_kernel, HEADS, head_size, side, attention, units),
            grid=(each,),
            in_specs=[
                at(two, width),
                at(two, wide, side),
                at(two, 128),
            ]
            + in_place(attention.arrays + begun),
            out_specs=at(two, wide),
            out_shape=sds((rows, wide), low),
            scratch_shapes=[
                pltpu.VMEM((two, width // 2), low),
                pltpu.VMEM((width // 2, width), low),
                pltpu.SemaphoreType.DMA((16,)),
            ],
            input_output_aliases={len(operands) - 1: 0} if begun else {},
            compiler_params=params(),
            cost_estimate=cost(12),
        )(*operands)

    def gradients(left, which, dtype, *came):
        block = pl.BlockSpec((side, width), lambda i: (i, 0))
        return pl.pallas_call(
            gradients_kernel,
            grid=(4,),
            in_specs=[
                pl.BlockSpec((rows, side), lambda i: (0, jnp.minimum(i, 2))),
                whole((rows, width)),
                pl.BlockSpec((side, width), lambda i: (which, 0)),
            ]
            + [block] * len(came),
            out_specs=block,
            out_shape=sds((4 * side, width), dtype),
            compiler_params=params(),
            cost_estimate=cost(8),
        )(left, normed, out_total, *came)

    d_last = attention_back(1, 1, attention_back(1, 0, None))
    near_send = gradients(d_last, 1, low)
    near_got = swap(near_send, *last)
    d_lead = attention_back(0, 1, attention_back(0, 0, None))
    for step_a, step_b in zip(steps_a, steps_b):
        up_held = reduce_step(up_held, step_a, 0, 1)
        down_held = reduce_step(down_held, step_b, 0, 1)
    feed_sum = sum_over_ctx(jnp.concatenate([up_held[0], down_held[0]], axis=0))

    shape = (2, half, units, width)
    lead_total = gradients(d_lead, 0, full, near_got)
    a_held = lead_total[: 2 * side].reshape(shape)
    b_held = lead_total[2 * side :].reshape(shape)

    input_grad, first_terms = pl.pallas_call(
        functools.partial(input_kernel, attention, units),
        name="input_gradient",
        grid=(block_count // 2,),
        in_specs=[
            rows_of(two, width),
            rows_of(two, width),
            rows_of(two, wide),
            rows_of(two, wide),
            whole((8, width)),
        ]
        + in_place(attention.arrays),
        out_specs=[resident_two, whole((8, width))],
        out_shape=[sds(frames_in.shape, full), sds((8, width), full)],
        scratch_shapes=[
            pltpu.VMEM((3 * width, width), low),
            pltpu.SemaphoreType.DMA((64,)),
        ],
        compiler_params=params(),
        cost_estimate=cost(14),
    )(tokens, hidden_low, d_lead, d_last, norms, *attention.arrays)

    for step_a, step_b in zip(steps_a, steps_b):
        a_held = reduce_step(a_held, step_a, 1, 3)
        b_held = reduce_step(b_held, step_b, 1, 3)
    norm_terms = sum_over(
        jnp.where(
            lax.broadcasted_iota(jnp.int32, first_terms.shape, 0) < 2, first_terms, second_terms
        ),
        ("tp", "fsdp", "ctx"),
    )
    norm_terms = lax.dynamic_slice_in_dim(
        norm_terms, lax.axis_index("fsdp") * part, part, 1
    )
    near_sum = sum_over_ctx(
        jnp.concatenate([a_held.reshape(-1, part), b_held.reshape(-1, part)], axis=0),
    )
    return (
        block_out,
        input_grad,
        near_sum[:units].T,
        near_sum[units : 2 * units].T,
        near_sum[2 * units : 3 * units].T,
        near_sum[3 * units :],
        feed_sum[:part],
        feed_sum[part:].T,
        norm_terms[0],
        norm_terms[1],
        norm_terms[2],
        norm_terms[3],
    )


def solution(mesh):
    tokens = P(None, ("fsdp", "ctx", "tp"), None)
    weights = (
        P("fsdp", "tp"),
        P("fsdp", "tp"),
        P("fsdp", "tp"),
        P("tp", "fsdp"),
        P("fsdp", "tp"),
        P("tp", "fsdp"),
        P("fsdp"),
        P("fsdp"),
        P("fsdp"),
        P("fsdp"),
    )
    return jax.shard_map(
        on_device,
        mesh=mesh,
        in_specs=(tokens, tokens) + weights,
        out_specs=(tokens, tokens) + weights,
        check_vma=False,
    )
```

time: 439 us -> 426 us (0.970)
  matrix products: 17.8 us -> 0 us
  Pallas kernels: 182 us -> 196 us
  local copies, waits for them, and re-layouts: 29 us -> 15.5 us
  waiting for transfers between devices: 146 us -> 153 us
  other arithmetic: 23.1 us -> 18.1 us
    pallas_call x1 -> x5, Pallas kernels: 5.16 us -> 34.1 us  [the longest x2 16.2 us: gradients(): pl.pallas_call(gradients_kernel, grid=(4,), in_specs=[pl.BlockSpec((rows,...]
    dot_general x3 -> x0, matrix products: 17.8 us -> none  [dot_left_t(): lax.dot_general(left, right, (((0,), (0,)), ((), ())), preferred_element_...]
    pallas_call x2 -> x0, local copies, waits for them, and re-layouts: 9.13 us -> none  [the longest x1 4.63 us: on_device(): pl.pallas_call(functools.partial(pad_kernel, frames_each), name='pad_fram...]
    pallas_call x1, Pallas kernels: 71.3 us -> 64 us  [on_device(): pl.pallas_call(functools.partial(forward_kernel, block_rows, feed, hidden...]
    ppermute x38 -> x40, waiting for transfers between devices: 146 us -> 153 us  [swap(): return lax.ppermute(block, axis, [(i, i ^ mask) for i in range(count)])]
    unnamed x64 -> x40, local copies, waits for them, and re-layouts: 11.7 us -> 5.99 us
    add x6, other arithmetic: 5.8 us -> 0.78 us  [reduce_step(): keep + swap(sent.astype(jnp.bfloat16), axis, mask).astype(jnp.float32)]
    pallas_call x1, Pallas kernels: 33.4 us -> 28.9 us  [on_device(): pl.pallas_call(functools.partial(attend_kernel, HEADS, head_size, attenti...]
  transfers between devices with their start and end apart: 38 -> 40, of which waited for: 18 -> 18; matrix products, arithmetic and copies ran while one was open for 12% -> 6% of each run, Pallas kernels for 25% -> 31%
where the time goes in v1:
time: 426 us; the launch traced here: 419 us
  Pallas kernels  196 us (46%)
  waiting for transfers between devices  153 us (36%)
  starting transfers between devices  34.8 us (8%)
  other arithmetic  18.1 us (4%)
  local copies, waits for them, and re-layouts  15.5 us (4%)
    ppermute x40, waiting for transfers between devices, swap(): return lax.ppermute(block, axis, [(i, i ^ mask) for i in range(count)])  153 us
    pallas_call x1, Pallas kernels, on_device(): pl.pallas_call(functools.partial(forward_kernel, block_rows, feed, hidden...  64 us
    pallas_call x4, Pallas kernels, attention_back(): pl.pallas_call(functools.partial(backward_kernel, HEADS, head_size, side,...  47.5 us
    ppermute x40, starting transfers between devices, swap(): return lax.ppermute(block, axis, [(i, i ^ mask) for i in range(count)])  34.8 us
    pallas_call x1, Pallas kernels, on_device(): pl.pallas_call(functools.partial(attend_kernel, HEADS, head_size, attenti...  28.9 us
    pallas_call x1, Pallas kernels, on_device(): pl.pallas_call(functools.partial(input_kernel, attention, units), name='i...  17.3 us
    pallas_call x2, Pallas kernels, gradients(): pl.pallas_call(gradients_kernel, grid=(4,), in_specs=[pl.BlockSpec((rows,...  16.2 us
  transfers between devices with their start and end apart: 40, of which 18 were waited for; matrix products, arithmetic and copies ran while one was open for 6% of the time, Pallas kernels for 31%

profile of v1, /device:TPU:0, one launch (start us, length us, event | category | flops | bytes accessed | tf_op | source)
XLA Modules:
  0.0 418.8 jit_solution(5444180102442288763)
XLA Ops:
  5.7 13.5 %collective-permute-done.1.refs_4_.gate_ref.refs_6_ = bf16[768,384]{1,0:T(8,128)(2,1)S(1)} collective-permute-done((bf16[768,384]{1,0:T(8,128)(2,1)}, bf16[768,384]{1,0:T(8,128)(2,1)S(1)}, u32[]{:S(2)}, u32[]{:S(2)}) %collective-permute-start.1) | collective-permute-done | bytes 589856 | tf_op jit(solution)/shard_map/ppermute | solution.py:58
  29.8 36.3 %collective-permute-done.2.refs_5_.refs_7_ = bf16[768,384]{1,0:T(8,128)(2,1)} collective-permute-done((bf16[768,384]{1,0:T(8,128)(2,1)S(1)}, bf16[768,384]{1,0:T(8,128)(2,1)}, u32[]{:S(2)}, u32[]{:S(2)}) %collective-permute-start.2) | collective-permute-done | bytes 589856 | tf_op jit(solution)/shard_map/ppermute | solution.py:58
  71.5 5.1 %collective-permute-done.4.refs_7_.refs_9_ = bf16[384,384]{1,0:T(8,128)(2,1)} collective-permute-done((bf16[384,384]{1,0:T(8,128)(2,1)S(1)}, bf16[384,384]{1,0:T(8,128)(2,1)}, u32[]{:S(2)}, u32[]{:S(2)}) %collective-permute-start.4) | collective-permute-done | bytes 294944 | tf_op jit(solution)/shard_map/ppermute | solution.py:58
  80.4 8.3 %prepare.1 = (bf16[1664,768]{1,0:T(8,128)(2,1)}, bf16[1664,768]{1,0:T(8,128)(2,1)}, bf16[768,1664]{1,0:T(8,128)(2,1)}, bf16[1664,768]{1,0:T(8,128)(2,1)}) custom-call(bf16[4,392,768]{2,1,0:T(8,128)(2,1)} %x_ref.1, bf16[4,392,768]{2,1,0:T(8,128)(2,1)} %g_ref.1, f32[8,768]{1,0:T(8,128)} %fusion.15.norm_ref.refs_2_.refs_5_.refs_4_), custom_call_target="tpu_custom_call" | custom-call | flops 9900000256 | tf_op jit(solution)/shard_map/prepare/pallas_call | solution.py:722
  89.4 4.2 collective-permute-done.12.refs_9_
  94.9 28.9 %attend.1 = (bf16[1664,2304]{1,0:T(8,128)(2,1)}, bf16[1664,768]{1,0:T(8,128)(2,1)}, f32[1664,128]{1,0:T(8,128)}, f32[1664,768]{1,0:T(8,128)}, bf16[1664,768]{1,0:T(8,128)(2,1)}) custom-call(bf16[1664,768]{1,0:T(8,128)(2,1)} %get-tuple-element.28.refs_0_, bf16[1664,768]{1,0:T(8,128)(2,1)} %get-tuple-element.29.refs_1_.right_ref, ...), custom_call_target="tpu_custom_call" | custom-call | flops 32999999488 | tf_op jit(solution)/shard_map/attend/pallas_call | solution.py:735
  123.8 4.0 turn.1.refs_2_
  128.8 64.0 %feed_forward.1 = (bf16[4,392,768]{2,1,0:T(8,128)(2,1)}, bf16[1664,768]{1,0:T(8,128)(2,1)}, f32[2,2,768,768]{3,2,1,0:T(8,128)}, bf16[2,2,768,768]{3,2,1,0:T(8,128)(2,1)}, f32[8,768]{1,0:T(8,128)}) custom-call(bf16[1664,768]{1,0:T(8,128)(2,1)} %get-tuple-element.30.source_ref.refs_0_, bf16[1664,768]{1,0:T(8,128)(2,1)} %get-tuple-element.31.refs_1_, ...), custom_call_target="tpu_custom_call" | custom-call | flops 68200001536 | tf_op jit(solution)/shard_map/feed_forward/pallas_call | solution.py:776
  193.4 11.8 %shard_map.213.refs_13_ = bf16[1664,1152]{1,0:T(8,128)(2,1)} custom-call(bf16[1664,768]{1,0:T(8,128)(2,1)} %get-tuple-element.35.refs_0_.refs_1_.right_ref, bf16[1664,2304]{1,0:T(8,128)(2,1)} %get-tuple-element.36.refs_1_, f32[1664,128]{1,0:T(8,128)} %get-tuple-element.37.refs_2_, bf16[768,384]{1,0:T(8,128)(2,1)} %pack_near.1.refs_3_.refs_5_, ...), custom_call_target="tpu_custom_call" | custom-call | flops 13200000000 | tf_op jit(solution)/shard_map/pallas_call | solution.py:848
  205.2 12.0 %shard_map.214.refs_3_.left_ref = bf16[1664,1152]{1,0:T(8,128)(2,1)} custom-call(bf16[1664,768]{1,0:T(8,128)(2,1)} %get-tuple-element.35.refs_0_.refs_1_.right_ref, bf16[1664,2304]{1,0:T(8,128)(2,1)} %get-tuple-element.36.refs_1_, f32[1664,128]{1,0:T(8,128)} %get-tuple-element.37.refs_2_, ...), custom_call_target="tpu_custom_call", output_to_operand_aliasing={{}: (13, {})} | custom-call | flops 13200000000 | tf_op jit(solution)/shard_map/pallas_call | solution.py:848
  217.3 5.7 %out_gradient.1.other_ref = f32[768,768]{1,0:T(8,128)} custom-call(bf16[1664,768]{1,0:T(8,128)(2,1)} %get-tuple-element.39.left_ref, bf16[1664,768]{1,0:T(8,128)(2,1)} %get-tuple-element.35.refs_0_.refs_1_.right_ref), custom_call_target="tpu_custom_call" | custom-call | flops 4400000000 | tf_op jit(solution)/shard_map/out_gradient/pallas_call | solution.py:824
  223.0 7.6 %shard_map.215 = bf16[1536,768]{1,0:T(8,128)(2,1)} custom-call(bf16[1664,1152]{1,0:T(8,128)(2,1)} %shard_map.214.refs_3_.left_ref, bf16[1664,768]{1,0:T(8,128)(2,1)} %get-tuple-element.29.refs_1_.right_ref, f32[768,768]{1,0:T(8,128)} %out_gradient.1.other_ref), custom_call_target="tpu_custom_call" | custom-call | flops 8800000000 | tf_op jit(solution)/shard_map/pallas_call | solution.py:871
  230.6 11.8 %shard_map.211.refs_13_ = bf16[1664,1152]{1,0:T(8,128)(2,1)} custom-call(bf16[1664,768]{1,0:T(8,128)(2,1)} %get-tuple-element.35.refs_0_.refs_1_.right_ref, bf16[1664,2304]{1,0:T(8,128)(2,1)} %get-tuple-element.36.refs_1_, f32[1664,128]{1,0:T(8,128)} %get-tuple-element.37.refs_2_, bf16[768,384]{1,0:T(8,128)(2,1)} %pack_near.1.refs_3_.refs_5_, ...), custom_call_target="tpu_custom_call" | custom-call | flops 13200000000 | tf_op jit(solution)/shard_map/pallas_call | solution.py:848
  242.4 11.9 %shard_map.212.refs_2_.left_ref = bf16[1664,1152]{1,0:T(8,128)(2,1)} custom-call(bf16[1664,768]{1,0:T(8,128)(2,1)} %get-tuple-element.35.refs_0_.refs_1_.right_ref, bf16[1664,2304]{1,0:T(8,128)(2,1)} %get-tuple-element.36.refs_1_, f32[1664,128]{1,0:T(8,128)} %get-tuple-element.37.refs_2_, ...), custom_call_target="tpu_custom_call", output_to_operand_aliasing={{}: (13, {})} | custom-call | flops 13200000000 | tf_op jit(solution)/shard_map/pallas_call | solution.py:848
  255.7 8.6 %shard_map.216 = f32[1536,768]{1,0:T(8,128)} custom-call(bf16[1664,1152]{1,0:T(8,128)(2,1)} %shard_map.212.refs_2_.left_ref, bf16[1664,768]{1,0:T(8,128)(2,1)} %get-tuple-element.29.refs_1_.right_ref, f32[768,768]{1,0:T(8,128)} %out_gradient.1.other_ref, bf16[1536,768]{1,0:T(8,128)(2,1)} %copy-done.13), custom_call_target="tpu_custom_call" | custom-call | flops 8800000000 | tf_op jit(solution)/shard_map/pallas_call | solution.py:871
  268.4 5.8 %convert_add_fusion = (f32[2,1,768,768]{3,2,1,0:T(8,128)S(1)}, f32[2,1,768,768]{3,2,1,0:T(8,128)S(1)}) fusion(f32[2,2,768,768]{3,2,1,0:T(8,128)} %get-tuple-element.40, bf16[2,2,768,768]{3,2,1,0:T(8,128)(2,1)} %collective-permute-done.27), kind=kLoop, calls=%fused_computation | loop fusion | flops 4718592 | bytes 23592960 | tf_op jit(solution)/shard_map/add | solution.py:835
  277.4 5.9 %collective-permute-done.22 = bf16[2,2,192,384]{3,2,1,0:T(8,128)(2,1)S(1)} collective-permute-done((bf16[2,2,192,384]{3,2,1,0:T(8,128)(2,1)S(1)}, bf16[2,2,192,384]{3,2,1,0:T(8,128)(2,1)S(1)}, u32[]{:S(2)}, u32[]{:S(2)}) %collective-permute-start.22) | collective-permute-done | bytes 589856 | tf_op jit(solution)/shard_map/ppermute | solution.py:58
  285.7 29.1 %collective-permute-done.23 = bf16[2,1,192,384]{3,2,1,0:T(8,128)(2,1)S(1)} collective-permute-done((bf16[2,1,192,384]{3,2,1,0:T(8,128)(2,1)S(1)}, bf16[2,1,192,384]{3,2,1,0:T(8,128)(2,1)S(1)}, u32[]{:S(2)}, u32[]{:S(2)}) %collective-permute-start.23) | collective-permute-done | bytes 294944 | tf_op jit(solution)/shard_map/ppermute | solution.py:58
  320.2 9.6 %collective-permute-done.31 = bf16[1,384,768]{2,1,0:T(8,128)(2,1)S(1)} collective-permute-done((bf16[1,384,768]{2,1,0:T(8,128)(2,1)S(1)}, bf16[1,384,768]{2,1,0:T(8,128)(2,1)S(1)}, u32[]{:S(2)}, u32[]{:S(2)}) %collective-permute-start.31) | collective-permute-done | bytes 589856 | tf_op jit(solution)/shard_map/ppermute | solution.py:58
  333.1 17.3 %input_gradient.1 = (f32[4,392,768]{2,1,0:T(8,128)}, f32[8,768]{1,0:T(8,128)}) custom-call(bf16[1664,768]{1,0:T(8,128)(2,1)} %get-tuple-element.28.refs_0_, bf16[1664,768]{1,0:T(8,128)(2,1)} %get-tuple-element.35.refs_0_.refs_1_.right_ref, bf16[1664,1152]{1,0:T(8,128)(2,1)} %shard_map.212.refs_2_.left_ref, bf16[1664,1152]{1,0:T(8,128)(2,1)} %shard_map.214.refs_3_.left_ref, ...), custom_call_target="tpu_custom_call" | custom-call | flops 15399999488 | tf_op jit(solution)/shard_map/input_gradient/pallas_call | solution.py:900
  367.3 6.0 %collective-permute-done.38 = f32[8,768]{1,0:T(8,128)} collective-permute-done((f32[8,768]{1,0:T(8,128)}, f32[8,768]{1,0:T(8,128)}, u32[]{:S(2)}, u32[]{:S(2)}) %collective-permute-start.38) | collective-permute-done | bytes 24608 | tf_op jit(solution)/shard_map/ppermute | solution.py:58
  375.2 17.7 %collective-permute-done.25 = bf16[384,384]{1,0:T(8,128)(2,1)} collective-permute-done((bf16[384,384]{1,0:T(8,128)(2,1)}, bf16[384,384]{1,0:T(8,128)(2,1)}, u32[]{:S(2)}, u32[]{:S(2)}) %collective-permute-start.25) | collective-permute-done | bytes 294944 | tf_op jit(solution)/shard_map/ppermute | solution.py:58
  398.7 5.5 %collective-permute-done.26 = bf16[384,384]{1,0:T(8,128)(2,1)S(1)} collective-permute-done((bf16[384,384]{1,0:T(8,128)(2,1)S(1)}, bf16[384,384]{1,0:T(8,128)(2,1)S(1)}, u32[]{:S(2)}, u32[]{:S(2)}) %collective-permute-start.26) | collective-permute-done | bytes 294944 | tf_op jit(solution)/shard_map/ppermute | solution.py:58
  405.3 10.4 %collective-permute-done.34 = bf16[384,768]{1,0:T(8,128)(2,1)S(1)} collective-permute-done((bf16[384,768]{1,0:T(8,128)(2,1)S(1)}, bf16[384,768]{1,0:T(8,128)(2,1)S(1)}, u32[]{:S(2)}, u32[]{:S(2)}) %collective-permute-start.34) | collective-permute-done | bytes 589856 | tf_op jit(solution)/shard_map/ppermute | solution.py:58
  (158 shorter events, 76.5 us)
Async XLA Ops:
  2.7 16.6 %collective-permute-start.1 = (bf16[768,384]{1,0:T(8,128)(2,1)}, bf16[768,384]{1,0:T(8,128)(2,1)S(1)}, u32[]{:S(2)}, u32[]{:S(2)}) collective-permute-start(bf16[768,384]{1,0:T(8,128)(2,1)} %pack_near.1.refs_3_.refs_5_), channel_id=1, source_target_pairs={{0,16},{16,0},{1,17},{17,1},{2,18},{18,2},{3,19},{19,3},{4,20},{20... | collective-permute-start | bytes 1769480 | tf_op jit(solution)/shard_map/ppermute | solution.py:58
  22.6 48.3 %collective-permute-start.10 = (bf16[1536,384]{1,0:T(8,128)(2,1)}, bf16[1536,384]{1,0:T(8,128)(2,1)S(1)}, u32[]{:S(2)}, u32[]{:S(2)}) collective-permute-start(bf16[1536,384]{1,0:T(8,128)(2,1)} %pack_feed.1.refs_6_), channel_id=1, source_target_pairs={{0,16},{16,0},{1,17},{17,1},{2,18},{18,2},{3,19},{19,3},{4,20},{20... | collective-permute-start | bytes 3538952 | tf_op jit(solution)/shard_map/ppermute | solution.py:58
  24.3 52.3 %collective-permute-start.11 = (bf16[1536,384]{1,0:T(8,128)(2,1)}, bf16[1536,384]{1,0:T(8,128)(2,1)}, u32[]{:S(2)}, u32[]{:S(2)}) collective-permute-start(bf16[1536,384]{1,0:T(8,128)(2,1)} %pack_feed.1.refs_6_), channel_id=1, source_target_pairs={{0,2},{1,3},{2,0},{3,1},{4,6},{5,7},{6,4},{7,5},{8,10},{9,11},{10,... | collective-permute-start | bytes 3538952 | tf_op jit(solution)/shard_map/ppermute | solution.py:58
  25.8 40.3 %collective-permute-start.2 = (bf16[768,384]{1,0:T(8,128)(2,1)S(1)}, bf16[768,384]{1,0:T(8,128)(2,1)}, u32[]{:S(2)}, u32[]{:S(2)}) collective-permute-start(bf16[768,384]{1,0:T(8,128)(2,1)S(1)} %copy-done.4), channel_id=1, source_target_pairs={{0,2},{1,3},{2,0},{3,1},{4,6},{5,7},{6,4},{7,5},{8,10},{9,11},{10,... | collective-permute-start | bytes 1769480 | tf_op jit(solution)/shard_map/ppermute | solution.py:58
  27.3 42.8 %collective-permute-start.3 = (bf16[384,384]{1,0:T(8,128)(2,1)S(1)}, bf16[384,384]{1,0:T(8,128)(2,1)}, u32[]{:S(2)}, u32[]{:S(2)}) collective-permute-start(bf16[384,384]{1,0:T(8,128)(2,1)S(1)} %slice.121), channel_id=1, source_target_pairs={{0,2},{1,3},{2,0},{3,1},{4,6},{5,7},{6,4},{7,5},{8,10},{9,11},{10,... | collective-permute-start | bytes 884744 | tf_op jit(solution)/shard_map/ppermute | solution.py:58
  28.9 49.3 %collective-permute-start.5 = (bf16[768,384]{1,0:T(8,128)(2,1)S(1)}, bf16[768,384]{1,0:T(8,128)(2,1)}, u32[]{:S(2)}, u32[]{:S(2)}) collective-permute-start(bf16[768,384]{1,0:T(8,128)(2,1)S(1)} %copy-done.4), channel_id=1, source_target_pairs={{0,1},{1,0},{2,3},{3,2},{4,5},{5,4},{6,7},{7,6},{8,9},{9,8},{10,11... | collective-permute-start | bytes 1769480 | tf_op jit(solution)/shard_map/ppermute | solution.py:58
  70.8 17.9 %collective-permute-start.6 = (bf16[768,384]{1,0:T(8,128)(2,1)S(1)}, bf16[768,384]{1,0:T(8,128)(2,1)}, u32[]{:S(2)}, u32[]{:S(2)}) collective-permute-start(bf16[768,384]{1,0:T(8,128)(2,1)S(1)} %copy-done.1), channel_id=1, source_target_pairs={{0,1},{1,0},{2,3},{3,2},{4,5},{5,4},{6,7},{7,6},{8,9},{9,8},{10,11... | collective-permute-start | bytes 1769480 | tf_op jit(solution)/shard_map/ppermute | solution.py:58
  88.7 39.1 %collective-permute-start.14 = (bf16[1536,384]{1,0:T(8,128)(2,1)S(1)}, bf16[1536,384]{1,0:T(8,128)(2,1)}, u32[]{:S(2)}, u32[]{:S(2)}) collective-permute-start(bf16[1536,384]{1,0:T(8,128)(2,1)S(1)} %copy-done.2), channel_id=1, source_target_pairs={{0,1},{1,0},{2,3},{3,2},{4,5},{5,4},{6,7},{7,6},{8,9},{9,8},{10,11... | collective-permute-start | bytes 3538952 | tf_op jit(solution)/shard_map/ppermute | solution.py:58
  88.8 39.0 %collective-permute-start.15 = (bf16[1536,384]{1,0:T(8,128)(2,1)}, bf16[1536,384]{1,0:T(8,128)(2,1)}, u32[]{:S(2)}, u32[]{:S(2)}) collective-permute-start(bf16[1536,384]{1,0:T(8,128)(2,1)} %copy-done.5), channel_id=1, source_target_pairs={{0,1},{1,0},{2,3},{3,2},{4,5},{5,4},{6,7},{7,6},{8,9},{9,8},{10,11... | collective-permute-start | bytes 3538952 | tf_op jit(solution)/shard_map/ppermute | solution.py:58
  89.3 38.5 %collective-permute-start.16 = (bf16[1536,384]{1,0:T(8,128)(2,1)}, bf16[1536,384]{1,0:T(8,128)(2,1)}, u32[]{:S(2)}, u32[]{:S(2)}) collective-permute-start(bf16[1536,384]{1,0:T(8,128)(2,1)} %collective-permute-done.11.refs_8_), channel_id=1, source_target_pairs={{0,1},{1,0},{2,3},{3,2},{4,5},{5,4},{6,7},{7,6},{8,9},{9,8},{10,11... | collective-permute-start | bytes 3538952 | tf_op jit(solution)/shard_map/ppermute | solution.py:58
  93.6 34.2 %collective-permute-start.17 = (bf16[768,384]{1,0:T(8,128)(2,1)S(1)}, bf16[768,384]{1,0:T(8,128)(2,1)S(1)}, u32[]{:S(2)}, u32[]{:S(2)}) collective-permute-start(bf16[768,384]{1,0:T(8,128)(2,1)S(1)} %collective-permute-done.12.refs_9_), channel_id=1, source_target_pairs={{0,1},{1,0},{2,3},{3,2},{4,5},{5,4},{6,7},{7,6},{8,9},{9,8},{10,11... | collective-permute-start | bytes 1769480 | tf_op jit(solution)/shard_map/ppermute | solution.py:58
  94.9 32.9 %collective-permute-start.18 = (bf16[768,384]{1,0:T(8,128)(2,1)}, bf16[768,384]{1,0:T(8,128)(2,1)S(1)}, u32[]{:S(2)}, u32[]{:S(2)}) collective-permute-start(bf16[768,384]{1,0:T(8,128)(2,1)} %collective-permute-done.13.refs_10_), channel_id=1, source_target_pairs={{0,1},{1,0},{2,3},{3,2},{4,5},{5,4},{6,7},{7,6},{8,9},{9,8},{10,11... | collective-permute-start | bytes 1769480 | tf_op jit(solution)/shard_map/ppermute | solution.py:58
  192.9 75.6 %collective-permute-start.27 = (bf16[2,2,768,768]{3,2,1,0:T(8,128)(2,1)}, bf16[2,2,768,768]{3,2,1,0:T(8,128)(2,1)}, u32[]{:S(2)}, u32[]{:S(2)}) collective-permute-start(bf16[2,2,768,768]{3,2,1,0:T(8,128)(2,1)} %get-tuple-element.41), channel_id=1, source_target_pairs={{0,1},{1,0},{2,3},{3,2},{4,5},{5,4},{6,7},{7,6},{8,9},{9,8},{10,11... | collective-permute-start | bytes 14155784 | tf_op jit(solution)/shard_map/ppermute | solution.py:58
  230.6 23.7 %collective-permute-start.19 = (bf16[1536,768]{1,0:T(8,128)(2,1)}, bf16[1536,768]{1,0:T(8,128)(2,1)S(1)}, u32[]{:S(2)}, u32[]{:S(2)}) collective-permute-start(bf16[1536,768]{1,0:T(8,128)(2,1)} %shard_map.215), channel_id=1, source_target_pairs={{0,1},{1,0},{2,3},{3,2},{4,5},{5,4},{6,7},{7,6},{8,9},{9,8},{10,11... | collective-permute-start | bytes 7077896 | tf_op jit(solution)/shard_map/ppermute | solution.py:58
  274.3 40.5 %collective-permute-start.30 = (bf16[2,384,768]{2,1,0:T(8,128)(2,1)S(1)}, bf16[2,384,768]{2,1,0:T(8,128)(2,1)S(1)}, u32[]{:S(2)}, u32[]{:S(2)}) collective-permute-start(bf16[2,384,768]{2,1,0:T(8,128)(2,1)S(1)} %fusion.1), channel_id=1, source_target_pairs={{0,16},{16,0},{1,17},{17,1},{2,18},{18,2},{3,19},{19,3},{4,20},{20... | collective-permute-start | bytes 3538952 | tf_op jit(solution)/shard_map/ppermute | solution.py:58
  276.0 39.6 %collective-permute-start.28 = (bf16[1,768,768]{2,1,0:T(8,128)(2,1)S(1)}, bf16[1,768,768]{2,1,0:T(8,128)(2,1)S(1)}, u32[]{:S(2)}, u32[]{:S(2)}) collective-permute-start(bf16[1,768,768]{2,1,0:T(8,128)(2,1)S(1)} %fusion.2), channel_id=1, source_target_pairs={{0,2},{1,3},{2,0},{3,1},{4,6},{5,7},{6,4},{7,5},{8,10},{9,11},{10,... | collective-permute-start | bytes 3538952 | tf_op jit(solution)/shard_map/ppermute | solution.py:58
  283.5 31.3 %collective-permute-start.23 = (bf16[2,1,192,384]{3,2,1,0:T(8,128)(2,1)S(1)}, bf16[2,1,192,384]{3,2,1,0:T(8,128)(2,1)S(1)}, u32[]{:S(2)}, u32[]{:S(2)}) collective-permute-start(bf16[2,1,192,384]{3,2,1,0:T(8,128)(2,1)S(1)} %slice.175), channel_id=1, source_target_pairs={{0,2},{1,3},{2,0},{3,1},{4,6},{5,7},{6,4},{7,5},{8,10},{9,11},{10,... | collective-permute-start | bytes 884744 | tf_op jit(solution)/shard_map/ppermute | solution.py:58
  284.4 33.2 %collective-permute-start.21 = (bf16[2,1,192,384]{3,2,1,0:T(8,128)(2,1)S(1)}, bf16[2,1,192,384]{3,2,1,0:T(8,128)(2,1)S(1)}, u32[]{:S(2)}, u32[]{:S(2)}) collective-permute-start(bf16[2,1,192,384]{3,2,1,0:T(8,128)(2,1)S(1)} %dynamic-slice_convert_fusion.3), channel_id=1, source_target_pairs={{0,16},{16,0},{1,17},{17,1},{2,18},{18,2},{3,19},{19,3},{4,20},{20... | collective-permute-start | bytes 884744 | tf_op jit(solution)/shard_map/ppermute | solution.py:58
  318.6 36.8 %collective-permute-start.24 = (bf16[384,384]{1,0:T(8,128)(2,1)}, bf16[384,384]{1,0:T(8,128)(2,1)S(1)}, u32[]{:S(2)}, u32[]{:S(2)}) collective-permute-start(bf16[384,384]{1,0:T(8,128)(2,1)} %fusion.9), channel_id=1, source_target_pairs={{0,4},{4,0},{8,12},{12,8},{1,5},{5,1},{9,13},{13,9},{2,6},{6,2},{1... | collective-permute-start | bytes 884744 | tf_op jit(solution)/shard_map/ppermute | solution.py:58
  331.5 19.0 %collective-permute-start.32 = (bf16[384,768]{1,0:T(8,128)(2,1)}, bf16[384,768]{1,0:T(8,128)(2,1)}, u32[]{:S(2)}, u32[]{:S(2)}) collective-permute-start(bf16[384,768]{1,0:T(8,128)(2,1)} %fusion.4), channel_id=1, source_target_pairs={{0,4},{4,0},{8,12},{12,8},{1,5},{5,1},{9,13},{13,9},{2,6},{6,2},{1... | collective-permute-start | bytes 1769480 | tf_op jit(solution)/shard_map/ppermute | solution.py:58
  352.8 41.5 %collective-permute-start.33 = (bf16[384,768]{1,0:T(8,128)(2,1)}, bf16[384,768]{1,0:T(8,128)(2,1)}, u32[]{:S(2)}, u32[]{:S(2)}) collective-permute-start(bf16[384,768]{1,0:T(8,128)(2,1)} %fusion.17), channel_id=1, source_target_pairs={{0,8},{4,12},{8,0},{12,4},{1,9},{5,13},{9,1},{13,5},{2,10},{6,14},... | collective-permute-start | bytes 1769480 | tf_op jit(solution)/shard_map/ppermute | solution.py:58
  357.0 35.9 %collective-permute-start.25 = (bf16[384,384]{1,0:T(8,128)(2,1)}, bf16[384,384]{1,0:T(8,128)(2,1)}, u32[]{:S(2)}, u32[]{:S(2)}) collective-permute-start(bf16[384,384]{1,0:T(8,128)(2,1)} %fusion.16), channel_id=1, source_target_pairs={{0,8},{4,12},{8,0},{12,4},{1,9},{5,13},{9,1},{13,5},{2,10},{6,14},... | collective-permute-start | bytes 884744 | tf_op jit(solution)/shard_map/ppermute | solution.py:58
  374.1 23.9 %collective-permute-start.39 = (f32[8,768]{1,0:T(8,128)S(1)}, f32[8,768]{1,0:T(8,128)S(1)}, u32[]{:S(2)}, u32[]{:S(2)}) collective-permute-start(f32[8,768]{1,0:T(8,128)S(1)} %add.105), channel_id=1, source_target_pairs={{0,8},{4,12},{8,0},{12,4},{1,9},{5,13},{9,1},{13,5},{2,10},{6,14},... | collective-permute-start | bytes 73736 | tf_op jit(solution)/shard_map/ppermute | solution.py:58
  396.0 19.7 %collective-permute-start.34 = (bf16[384,768]{1,0:T(8,128)(2,1)S(1)}, bf16[384,768]{1,0:T(8,128)(2,1)S(1)}, u32[]{:S(2)}, u32[]{:S(2)}) collective-permute-start(bf16[384,768]{1,0:T(8,128)(2,1)S(1)} %get-tuple-element.60), channel_id=1, source_target_pairs={{0,4},{4,0},{8,12},{12,8},{1,5},{5,1},{9,13},{13,9},{2,6},{6,2},{1... | collective-permute-start | bytes 1769480 | tf_op jit(solution)/shard_map/ppermute | solution.py:58
  (34 other events, 410.4 us)

commit v2 on v1

--- a/solution.py
+++ b/solution.py
@@ -257,8 +257,12 @@
 
 
 def turn(source, target):
-    for start in range(0, source.shape[0], 128):
-        target[:, start : start + 128] = source[start : start + 128, :].T
+    def one(n, carry):
+        part = pl.ds(pl.multiple_of(n * 128, 128), 128)
+        target[:, part] = source[part, :].T
+        return carry
+
+    lax.fori_loop(0, source.shape[0] // 128, one, 0)
 
 
 def turn_kernel(source_ref, target_ref):
@@ -412,18 +416,19 @@
     arrays, norm_ref = refs[:5], refs[5]
     raw = refs[6 : 6 + count]
     out_any, low_any, keep_any, send_ref, ngrad_ref = refs[6 + count : 11 + count]
-    held = refs[11 + count : 16 + count]
-    sn_ref, cot_ref, snt_ref, cott_ref, hidden_ref = held
+    held = refs[11 + count : 15 + count]
+    sn_ref, cot_ref, turned_ref, hidden_ref = held
     (
-        y_ref, dh_ref, act_ref, din_ref, next_ref, wup_ref, wdown_ref, wupt_ref, wdownt_ref,
+        y_ref, dh_ref, by_ref, next_ref, wup_ref, wdown_ref, wupt_ref, wdownt_ref,
         keep_ref, out_ref, low_ref, sems, held_sems, keep_sems, out_sems, low_sems,
-    ) = refs[16 + count :]
+    ) = refs[15 + count :]
     step, steps = pl.program_id(0), len(pack.pieces)
     tiles = sn_ref.shape[0] // tile
     chunk = sn_ref.shape[1] // tiles
     wide = 2 * tile
     order = [(n + steps // 2) % steps for n in range(steps)]
-    late = copies_on(zip(arrays, held), held_sems)
+    targets = (sn_ref, cot_ref, turned_ref.at[0], turned_ref.at[1], hidden_ref)
+    late = copies_on(zip(arrays, targets), held_sems)
 
     def copies_of(n):
         pairs = pack.copies(raw, order[n], 0, units, next_ref.at[0], 0)
@@ -465,8 +470,8 @@
         active = (inner * share).astype(jnp.bfloat16)
         slope = share + inner * (jnp.exp(-0.5 * inner * inner) * INV_ROOT_TAU)
         d_inner = (d_active * slope).astype(jnp.bfloat16)
-        act_ref[rows, :] = active
-        din_ref[rows, :] = d_inner
+        by_ref[1, rows, :] = active
+        by_ref[0, rows, :] = d_inner
         y_ref[rows, :] += dot_rows(active, wdown_ref[...])
         dh_ref[rows, :] += dot_rows(d_inner, wup_ref[...])
         return carry
@@ -477,9 +482,8 @@
     def _():
         wait_all(late[2:4])
 
-    def weight_gradients(rows):
-        keep_ref[0, rows, :] = dot_rows(snt_ref[rows, :], din_ref[...])
-        keep_ref[1, rows, :] = dot_rows(cott_ref[rows, :], act_ref[...])
+    def weight_gradient(n, rows):
+        keep_ref[n, rows, :] = dot_rows(turned_ref[n, rows, :], by_ref[n])
 
     def whole_keep(p):
         return pltpu.make_async_copy(
@@ -500,9 +504,12 @@
 
     @pl.when(step < steps - 1)
     def _():
-        weight_gradients(slice(None))
-        for n in range(2):
+        def one(n, carry):
+            weight_gradient(n, slice(None))
             settle(n, units // 2)
+            return carry
+
+        lax.fori_loop(0, 2, one, 0)
 
     @pl.when(step < steps // 2)
     def _():
@@ -539,7 +546,8 @@
             ]
 
         def close(n, carry):
-            weight_gradients(pl.ds(pl.multiple_of(n * chunk, 16), chunk))
+            for m in range(2):
+                weight_gradient(m, pl.ds(pl.multiple_of(n * chunk, 16), chunk))
             rows = pl.ds(pl.multiple_of(n * tile, 16), tile)
             hidden = hidden_ref[rows, :]
             out_ref[n] = unpad(hidden + y_ref[rows, :]).astype(jnp.bfloat16)
@@ -702,7 +710,6 @@
 
     near = pl.pallas_call(
         pack_near_kernel,
-        name="pack_near",
         out_shape=sds((4 * units, part), low),
         compiler_params=params(),
     )(w_query.T, w_key.T, w_value.T, w_out)
@@ -710,7 +717,6 @@
     norms = gather_columns([norm1_gain, norm1_bias, norm2_gain, norm2_bias]).astype(full)
     feed_here = pl.pallas_call(
         pack_feed_kernel,
-        name="pack_feed",
         in_specs=[pl.BlockSpec(memory_space=pltpu.VMEM)] * 2
         + [pl.BlockSpec(memory_space=pl.ANY)],
         out_shape=sds((2 * hidden_units, part), low),
@@ -721,7 +727,6 @@
     resident_two = pl.BlockSpec((2, resident_rows, width), lambda i: (i, 0, 0))
     tokens, cotangent, cotangent_t, normed = pl.pallas_call(
         functools.partial(prepare_kernel, frames_each),
-        name="prepare",
         out_shape=[
             sds((rows, width), low),
             sds((rows, width), low),
@@ -734,7 +739,6 @@
 
     qkv, mixed, logs, hidden, second = pl.pallas_call(
         functools.partial(attend_kernel, HEADS, head_size, attention, units),
-        name="attend",
         grid=(block_count // 2,),
         in_specs=[rows_of(two, width), rows_of(two, width), whole((8, width))]
         + in_place(attention.arrays),
@@ -763,7 +767,6 @@
 
     second_t = pl.pallas_call(
         turn_kernel,
-        name="turn",
         out_shape=sds((width, rows), low),
         compiler_params=params(),
         cost_estimate=cost(5),
@@ -775,12 +778,11 @@
     )
     block_out, hidden_low, feed_keep, feed_send, second_terms = pl.pallas_call(
         functools.partial(forward_kernel, block_rows, feed, hidden_units),
-        name="feed_forward",
         grid=(pieces,),
         in_specs=in_place((second, cotangent, second_t, cotangent_t, hidden))
         + [whole((8, width))]
         + in_place(feed.arrays),
-        out_specs=in_place(("block_out", "hidden_low", "feed_keep"))
+        out_specs=in_place((0, 0, 0))
         + [send_block, whole((8, width))],
         out_shape=[
             sds(frames_in.shape, low),
@@ -792,13 +794,11 @@
         scratch_shapes=[
             pltpu.VMEM((rows, width), low),
             pltpu.VMEM((rows, width), low),
-            pltpu.VMEM((width, rows), low),
-            pltpu.VMEM((width, rows), low),
+            pltpu.VMEM((2, width, rows), low),
             pltpu.VMEM((rows, width), full),
             pltpu.VMEM((rows, width), full),
             pltpu.VMEM((rows, width), full),
-            pltpu.VMEM((rows, hidden_units), low),
-            pltpu.VMEM((rows, hidden_units), low),
+            pltpu.VMEM((2, rows, hidden_units), low),
             pltpu.VMEM((2, hidden_units, width), low),
             pltpu.VMEM((hidden_units, width), low),
             pltpu.VMEM((hidden_units, width), low),
@@ -823,7 +823,6 @@
     side = width // 2
     out_total = pl.pallas_call(
         gradient_kernel,
-        name="out_gradient",
         grid=(2,),
         in_specs=[pl.BlockSpec((rows, side), lambda i: (0, i)), whole((rows, width))],
         out_specs=rows_of(side, width),
@@ -836,15 +835,13 @@
 
     wide = 3 * width // 2
 
-    def attention_back(side, group, begun):
-        each = block_count // 4
-        base = group * each
+    def attention_back(side):
+        each = block_count // 2
 
         def at(count, columns, column=0):
-            return pl.BlockSpec((count, columns), lambda i: (base + i, column))
-
-        begun = () if begun is None else (begun,)
-        operands = (hidden_low, qkv, logs) + attention.arrays + begun
+            return pl.BlockSpec((count, columns), lambda i: (i, column))
+
+        operands = (hidden_low, qkv, logs) + attention.arrays
         return pl.pallas_call(
             functools.partial(backward_kernel, HEADS, head_size, side, attention, units),
             grid=(each,),
@@ -853,7 +850,7 @@
                 at(two, wide, side),
                 at(two, 128),
             ]
-            + in_place(attention.arrays + begun),
+            + in_place(attention.arrays),
             out_specs=at(two, wide),
             out_shape=sds((rows, wide), low),
             scratch_shapes=[
@@ -861,9 +858,8 @@
                 pltpu.VMEM((width // 2, width), low),
                 pltpu.SemaphoreType.DMA((16,)),
             ],
-            input_output_aliases={len(operands) - 1: 0} if begun else {},
             compiler_params=params(),
-            cost_estimate=cost(12),
+            cost_estimate=cost(24),
         )(*operands)
 
     def gradients(left, which, dtype, *came):
@@ -883,10 +879,10 @@
             cost_estimate=cost(8),
         )(left, normed, out_total, *came)
 
-    d_last = attention_back(1, 1, attention_back(1, 0, None))
+    d_last = attention_back(1)
     near_send = gradients(d_last, 1, low)
     near_got = swap(near_send, *last)
-    d_lead = attention_back(0, 1, attention_back(0, 0, None))
+    d_lead = attention_back(0)
     for step_a, step_b in zip(steps_a, steps_b):
         up_held = reduce_step(up_held, step_a, 0, 1)
         down_held = reduce_step(down_held, step_b, 0, 1)
@@ -899,7 +895,6 @@
 
     input_grad, first_terms = pl.pallas_call(
         functools.partial(input_kernel, attention, units),
-        name="input_gradient",
         grid=(block_count // 2,),
         in_specs=[
             rows_of(two, width),

time: 426 us -> 412 us (0.967); the launches traced: 419 us -> 411 us
  Pallas kernels: 196 us -> 190 us
    pallas_call x4 -> x2, Pallas kernels: 47.5 us -> 39.1 us  [attention_back(): pl.pallas_call(functools.partial(backward_kernel, HEADS, head_size, side,...]
  transfers between devices with their start and end apart: 40 -> 40, of which waited for: 18 -> 18; matrix products, arithmetic and copies ran while one was open for 6% -> 6% of each run, Pallas kernels for 31% -> 30%
where the time goes in v2:
time: 412 us; the launch traced here: 411 us
  Pallas kernels  190 us (46%)
  waiting for transfers between devices  151 us (37%)
  starting transfers between devices  34.8 us (8%)
  other arithmetic  17.9 us (4%)
  local copies, waits for them, and re-layouts  15.5 us (4%)
    ppermute x40, waiting for transfers between devices, swap(): return lax.ppermute(block, axis, [(i, i ^ mask) for i in range(count)])  151 us
    pallas_call x1, Pallas kernels, on_device(): pl.pallas_call(functools.partial(forward_kernel, block_rows, feed, hidden...  64.1 us
    pallas_call x2, Pallas kernels, attention_back(): pl.pallas_call(functools.partial(backward_kernel, HEADS, head_size, side,...  39.1 us
    ppermute x40, starting transfers between devices, swap(): return lax.ppermute(block, axis, [(i, i ^ mask) for i in range(count)])  34.8 us
    pallas_call x1, Pallas kernels, on_device(): pl.pallas_call(functools.partial(attend_kernel, HEADS, head_size, attenti...  28.9 us
    pallas_call x1, Pallas kernels, on_device(): pl.pallas_call(functools.partial(input_kernel, attention, units), grid=(b...  17.3 us
    pallas_call x2, Pallas kernels, gradients(): pl.pallas_call(gradients_kernel, grid=(4,), in_specs=[pl.BlockSpec((rows,...  16.2 us
    pallas_call x1, Pallas kernels, on_device(): pl.pallas_call(functools.partial(prepare_kernel, frames_each), out_shape=...  10 us
  transfers between devices with their start and end apart: 40, of which 18 were waited for; matrix products, arithmetic and copies ran while one was open for 6% of the time, Pallas kernels for 30%

profile of v2, /device:TPU:0, one launch (start us, length us, event | category | flops | bytes accessed | tf_op | source)
XLA Modules:
  0.0 411.0 jit_solution(4820346811584558525)
XLA Ops:
  2.7 3.0 collective-permute-start.1
  5.7 13.5 %collective-permute-done.1.refs_4_.gate_ref.refs_6_ = bf16[768,384]{1,0:T(8,128)(2,1)S(1)} collective-permute-done((bf16[768,384]{1,0:T(8,128)(2,1)}, bf16[768,384]{1,0:T(8,128)(2,1)S(1)}, u32[]{:S(2)}, u32[]{:S(2)}) %collective-permute-start.1) | collective-permute-done | bytes 589856 | tf_op jit(solution)/shard_map/ppermute | solution.py:58
  29.8 36.3 %collective-permute-done.2.refs_5_.refs_7_ = bf16[768,384]{1,0:T(8,128)(2,1)} collective-permute-done((bf16[768,384]{1,0:T(8,128)(2,1)S(1)}, bf16[768,384]{1,0:T(8,128)(2,1)}, u32[]{:S(2)}, u32[]{:S(2)}) %collective-permute-start.2) | collective-permute-done | bytes 589856 | tf_op jit(solution)/shard_map/ppermute | solution.py:58
  71.5 5.1 %collective-permute-done.4.refs_7_.refs_9_ = bf16[384,384]{1,0:T(8,128)(2,1)} collective-permute-done((bf16[384,384]{1,0:T(8,128)(2,1)S(1)}, bf16[384,384]{1,0:T(8,128)(2,1)}, u32[]{:S(2)}, u32[]{:S(2)}) %collective-permute-start.4) | collective-permute-done | bytes 294944 | tf_op jit(solution)/shard_map/ppermute | solution.py:58
  80.4 10.0 %shard_map.211 = (bf16[1664,768]{1,0:T(8,128)(2,1)}, bf16[1664,768]{1,0:T(8,128)(2,1)}, bf16[768,1664]{1,0:T(8,128)(2,1)}, bf16[1664,768]{1,0:T(8,128)(2,1)}) custom-call(bf16[4,392,768]{2,1,0:T(8,128)(2,1)} %x_ref.1, bf16[4,392,768]{2,1,0:T(8,128)(2,1)} %g_ref.1, f32[8,768]{1,0:T(8,128)} %fusion.15.norm_ref.refs_2_.refs_5_.refs_4_), custom_call_target="tpu_custom_call" | custom-call | flops 9900000256 | tf_op jit(solution)/shard_map/pallas_call | solution.py:728
  94.9 28.9 %shard_map.213 = (bf16[1664,2304]{1,0:T(8,128)(2,1)}, bf16[1664,768]{1,0:T(8,128)(2,1)}, f32[1664,128]{1,0:T(8,128)}, f32[1664,768]{1,0:T(8,128)}, bf16[1664,768]{1,0:T(8,128)(2,1)}) custom-call(bf16[1664,768]{1,0:T(8,128)(2,1)} %get-tuple-element.28.refs_0_, bf16[1664,768]{1,0:T(8,128)(2,1)} %get-tuple-element.29.refs_1_.right_ref, ...), custom_call_target="tpu_custom_call" | custom-call | flops 32999999488 | tf_op jit(solution)/shard_map/pallas_call | solution.py:740
  123.8 4.6 %shard_map.214.refs_2_ = bf16[768,1664]{1,0:T(8,128)(2,1)} custom-call(bf16[1664,768]{1,0:T(8,128)(2,1)} %get-tuple-element.30.source_ref.refs_0_), custom_call_target="tpu_custom_call" | custom-call | flops 5500000256 | tf_op jit(solution)/shard_map/pallas_call | solution.py:768
  129.5 64.1 %shard_map.216 = (bf16[4,392,768]{2,1,0:T(8,128)(2,1)}, bf16[1664,768]{1,0:T(8,128)(2,1)}, f32[2,2,768,768]{3,2,1,0:T(8,128)}, bf16[2,2,768,768]{3,2,1,0:T(8,128)(2,1)}, f32[8,768]{1,0:T(8,128)}) custom-call(bf16[1664,768]{1,0:T(8,128)(2,1)} %get-tuple-element.30.source_ref.refs_0_, bf16[1664,768]{1,0:T(8,128)(2,1)} %get-tuple-element.31.refs_1_, ...), custom_call_target="tpu_custom_call" | custom-call | flops 68200001536 | tf_op jit(solution)/shard_map/pallas_call | solution.py:779
  194.1 19.6 %shard_map.218.refs_3_.left_ref = bf16[1664,1152]{1,0:T(8,128)(2,1)} custom-call(bf16[1664,768]{1,0:T(8,128)(2,1)} %get-tuple-element.35.refs_0_.refs_1_.right_ref, bf16[1664,2304]{1,0:T(8,128)(2,1)} %get-tuple-element.36.refs_1_, f32[1664,128]{1,0:T(8,128)} %get-tuple-element.37.refs_2_, bf16[768,384]{1,0:T(8,128)(2,1)} %shard_map.212.refs_3_.refs_5_, ...), custom_call_target="tpu_custom_call" | custom-call | flops 26400000000 | tf_op jit(solution)/shard_map/pallas_call | solution.py:845
  213.7 5.7 %shard_map.220.other_ref = f32[768,768]{1,0:T(8,128)} custom-call(bf16[1664,768]{1,0:T(8,128)(2,1)} %get-tuple-element.39.left_ref, bf16[1664,768]{1,0:T(8,128)(2,1)} %get-tuple-element.35.refs_0_.refs_1_.right_ref), custom_call_target="tpu_custom_call" | custom-call | flops 4400000000 | tf_op jit(solution)/shard_map/pallas_call | solution.py:824
  219.4 7.6 %shard_map.221 = bf16[1536,768]{1,0:T(8,128)(2,1)} custom-call(bf16[1664,1152]{1,0:T(8,128)(2,1)} %shard_map.218.refs_3_.left_ref, bf16[1664,768]{1,0:T(8,128)(2,1)} %get-tuple-element.29.refs_1_.right_ref, f32[768,768]{1,0:T(8,128)} %shard_map.220.other_ref), custom_call_target="tpu_custom_call" | custom-call | flops 8800000000 | tf_op jit(solution)/shard_map/pallas_call | solution.py:867
  227.0 19.5 %shard_map.217.refs_2_.left_ref = bf16[1664,1152]{1,0:T(8,128)(2,1)} custom-call(bf16[1664,768]{1,0:T(8,128)(2,1)} %get-tuple-element.35.refs_0_.refs_1_.right_ref, bf16[1664,2304]{1,0:T(8,128)(2,1)} %get-tuple-element.36.refs_1_, f32[1664,128]{1,0:T(8,128)} %get-tuple-element.37.refs_2_, bf16[768,384]{1,0:T(8,128)(2,1)} %shard_map.212.refs_3_.refs_5_, ...), custom_call_target="tpu_custom_call" | custom-call | flops 26400000000 | tf_op jit(solution)/shard_map/pallas_call | solution.py:845
  247.9 8.6 %shard_map.222 = f32[1536,768]{1,0:T(8,128)} custom-call(bf16[1664,1152]{1,0:T(8,128)(2,1)} %shard_map.217.refs_2_.left_ref, bf16[1664,768]{1,0:T(8,128)(2,1)} %get-tuple-element.29.refs_1_.right_ref, f32[768,768]{1,0:T(8,128)} %shard_map.220.other_ref, bf16[1536,768]{1,0:T(8,128)(2,1)} %copy-done.13), custom_call_target="tpu_custom_call" | custom-call | flops 8800000000 | tf_op jit(solution)/shard_map/pallas_call | solution.py:867
  256.5 2.7 fusion.20
  260.6 5.5 %convert_add_fusion = (f32[2,1,768,768]{3,2,1,0:T(8,128)S(1)}, f32[2,1,768,768]{3,2,1,0:T(8,128)S(1)}) fusion(f32[2,2,768,768]{3,2,1,0:T(8,128)} %get-tuple-element.40, bf16[2,2,768,768]{3,2,1,0:T(8,128)(2,1)} %collective-permute-done.27), kind=kLoop, calls=%fused_computation | loop fusion | flops 4718592 | bytes 23592960 | tf_op jit(solution)/shard_map/add | solution.py:834
  269.4 6.1 %collective-permute-done.22 = bf16[2,2,192,384]{3,2,1,0:T(8,128)(2,1)S(1)} collective-permute-done((bf16[2,2,192,384]{3,2,1,0:T(8,128)(2,1)S(1)}, bf16[2,2,192,384]{3,2,1,0:T(8,128)(2,1)S(1)}, u32[]{:S(2)}, u32[]{:S(2)}) %collective-permute-start.22) | collective-permute-done | bytes 589856 | tf_op jit(solution)/shard_map/ppermute | solution.py:58
  277.9 29.2 %collective-permute-done.23 = bf16[2,1,192,384]{3,2,1,0:T(8,128)(2,1)S(1)} collective-permute-done((bf16[2,1,192,384]{3,2,1,0:T(8,128)(2,1)S(1)}, bf16[2,1,192,384]{3,2,1,0:T(8,128)(2,1)S(1)}, u32[]{:S(2)}, u32[]{:S(2)}) %collective-permute-start.23) | collective-permute-done | bytes 294944 | tf_op jit(solution)/shard_map/ppermute | solution.py:58
  312.4 9.7 %collective-permute-done.31 = bf16[1,384,768]{2,1,0:T(8,128)(2,1)S(1)} collective-permute-done((bf16[1,384,768]{2,1,0:T(8,128)(2,1)S(1)}, bf16[1,384,768]{2,1,0:T(8,128)(2,1)S(1)}, u32[]{:S(2)}, u32[]{:S(2)}) %collective-permute-start.31) | collective-permute-done | bytes 589856 | tf_op jit(solution)/shard_map/ppermute | solution.py:58
  325.5 17.3 %shard_map.219 = (f32[4,392,768]{2,1,0:T(8,128)}, f32[8,768]{1,0:T(8,128)}) custom-call(bf16[1664,768]{1,0:T(8,128)(2,1)} %get-tuple-element.28.refs_0_, bf16[1664,768]{1,0:T(8,128)(2,1)} %get-tuple-element.35.refs_0_.refs_1_.right_ref, bf16[1664,1152]{1,0:T(8,128)(2,1)} %shard_map.217.refs_2_.left_ref, bf16[1664,1152]{1,0:T(8,128)(2,1)} %shard_map.218.refs_3_.left_ref, ...), custom_call_target="tpu_custom_call" | custom-call | flops 15399999488 | tf_op jit(solution)/shard_map/pallas_call | solution.py:896
  345.1 2.6 collective-permute-start.33
  359.7 6.1 %collective-permute-done.38 = f32[8,768]{1,0:T(8,128)} collective-permute-done((f32[8,768]{1,0:T(8,128)}, f32[8,768]{1,0:T(8,128)}, u32[]{:S(2)}, u32[]{:S(2)}) %collective-permute-start.38) | collective-permute-done | bytes 24608 | tf_op jit(solution)/shard_map/ppermute | solution.py:58
  367.6 17.7 %collective-permute-done.25 = bf16[384,384]{1,0:T(8,128)(2,1)} collective-permute-done((bf16[384,384]{1,0:T(8,128)(2,1)}, bf16[384,384]{1,0:T(8,128)(2,1)}, u32[]{:S(2)}, u32[]{:S(2)}) %collective-permute-start.25) | collective-permute-done | bytes 294944 | tf_op jit(solution)/shard_map/ppermute | solution.py:58
  391.1 5.5 %collective-permute-done.26 = bf16[384,384]{1,0:T(8,128)(2,1)S(1)} collective-permute-done((bf16[384,384]{1,0:T(8,128)(2,1)S(1)}, bf16[384,384]{1,0:T(8,128)(2,1)S(1)}, u32[]{:S(2)}, u32[]{:S(2)}) %collective-permute-start.26) | collective-permute-done | bytes 294944 | tf_op jit(solution)/shard_map/ppermute | solution.py:58
  397.7 10.4 %collective-permute-done.34 = bf16[384,768]{1,0:T(8,128)(2,1)S(1)} collective-permute-done((bf16[384,768]{1,0:T(8,128)(2,1)S(1)}, bf16[384,768]{1,0:T(8,128)(2,1)S(1)}, u32[]{:S(2)}, u32[]{:S(2)}) %collective-permute-start.34) | collective-permute-done | bytes 589856 | tf_op jit(solution)/shard_map/ppermute | solution.py:58
  (156 shorter events, 70.7 us)
Async XLA Ops:
  2.7 16.6 %collective-permute-start.1 = (bf16[768,384]{1,0:T(8,128)(2,1)}, bf16[768,384]{1,0:T(8,128)(2,1)S(1)}, u32[]{:S(2)}, u32[]{:S(2)}) collective-permute-start(bf16[768,384]{1,0:T(8,128)(2,1)} %shard_map.212.refs_3_.refs_5_), channel_id=1, source_target_pairs={{0,16},{16,0},{1,17},{17,1},{2,18},{18,2},{3,19},{19,3},{4,20},{20... | collective-permute-start | bytes 1769480 | tf_op jit(solution)/shard_map/ppermute | solution.py:58
  22.6 48.3 %collective-permute-start.10 = (bf16[1536,384]{1,0:T(8,128)(2,1)}, bf16[1536,384]{1,0:T(8,128)(2,1)S(1)}, u32[]{:S(2)}, u32[]{:S(2)}) collective-permute-start(bf16[1536,384]{1,0:T(8,128)(2,1)} %shard_map.215.refs_6_), channel_id=1, source_target_pairs={{0,16},{16,0},{1,17},{17,1},{2,18},{18,2},{3,19},{19,3},{4,20},{20... | collective-permute-start | bytes 3538952 | tf_op jit(solution)/shard_map/ppermute | solution.py:58
  24.3 52.3 %collective-permute-start.11 = (bf16[1536,384]{1,0:T(8,128)(2,1)}, bf16[1536,384]{1,0:T(8,128)(2,1)}, u32[]{:S(2)}, u32[]{:S(2)}) collective-permute-start(bf16[1536,384]{1,0:T(8,128)(2,1)} %shard_map.215.refs_6_), channel_id=1, source_target_pairs={{0,2},{1,3},{2,0},{3,1},{4,6},{5,7},{6,4},{7,5},{8,10},{9,11},{10,... | collective-permute-start | bytes 3538952 | tf_op jit(solution)/shard_map/ppermute | solution.py:58
  25.8 40.3 %collective-permute-start.2 = (bf16[768,384]{1,0:T(8,128)(2,1)S(1)}, bf16[768,384]{1,0:T(8,128)(2,1)}, u32[]{:S(2)}, u32[]{:S(2)}) collective-permute-start(bf16[768,384]{1,0:T(8,128)(2,1)S(1)} %copy-done.4), channel_id=1, source_target_pairs={{0,2},{1,3},{2,0},{3,1},{4,6},{5,7},{6,4},{7,5},{8,10},{9,11},{10,... | collective-permute-start | bytes 1769480 | tf_op jit(solution)/shard_map/ppermute | solution.py:58
  27.3 42.8 %collective-permute-start.3 = (bf16[384,384]{1,0:T(8,128)(2,1)S(1)}, bf16[384,384]{1,0:T(8,128)(2,1)}, u32[]{:S(2)}, u32[]{:S(2)}) collective-permute-start(bf16[384,384]{1,0:T(8,128)(2,1)S(1)} %slice.121), channel_id=1, source_target_pairs={{0,2},{1,3},{2,0},{3,1},{4,6},{5,7},{6,4},{7,5},{8,10},{9,11},{10,... | collective-permute-start | bytes 884744 | tf_op jit(solution)/shard_map/ppermute | solution.py:58
  28.9 49.3 %collective-permute-start.5 = (bf16[768,384]{1,0:T(8,128)(2,1)S(1)}, bf16[768,384]{1,0:T(8,128)(2,1)}, u32[]{:S(2)}, u32[]{:S(2)}) collective-permute-start(bf16[768,384]{1,0:T(8,128)(2,1)S(1)} %copy-done.4), channel_id=1, source_target_pairs={{0,1},{1,0},{2,3},{3,2},{4,5},{5,4},{6,7},{7,6},{8,9},{9,8},{10,11... | collective-permute-start | bytes 1769480 | tf_op jit(solution)/shard_map/ppermute | solution.py:58
  70.8 19.7 %collective-permute-start.6 = (bf16[768,384]{1,0:T(8,128)(2,1)S(1)}, bf16[768,384]{1,0:T(8,128)(2,1)}, u32[]{:S(2)}, u32[]{:S(2)}) collective-permute-start(bf16[768,384]{1,0:T(8,128)(2,1)S(1)} %copy-done.1), channel_id=1, source_target_pairs={{0,1},{1,0},{2,3},{3,2},{4,5},{5,4},{6,7},{7,6},{8,9},{9,8},{10,11... | collective-permute-start | bytes 1769480 | tf_op jit(solution)/shard_map/ppermute | solution.py:58
  90.4 38.0 %collective-permute-start.14 = (bf16[1536,384]{1,0:T(8,128)(2,1)S(1)}, bf16[1536,384]{1,0:T(8,128)(2,1)}, u32[]{:S(2)}, u32[]{:S(2)}) collective-permute-start(bf16[1536,384]{1,0:T(8,128)(2,1)S(1)} %copy-done.2), channel_id=1, source_target_pairs={{0,1},{1,0},{2,3},{3,2},{4,5},{5,4},{6,7},{7,6},{8,9},{9,8},{10,11... | collective-permute-start | bytes 3538952 | tf_op jit(solution)/shard_map/ppermute | solution.py:58
  90.5 37.9 %collective-permute-start.15 = (bf16[1536,384]{1,0:T(8,128)(2,1)}, bf16[1536,384]{1,0:T(8,128)(2,1)}, u32[]{:S(2)}, u32[]{:S(2)}) collective-permute-start(bf16[1536,384]{1,0:T(8,128)(2,1)} %copy-done.5), channel_id=1, source_target_pairs={{0,1},{1,0},{2,3},{3,2},{4,5},{5,4},{6,7},{7,6},{8,9},{9,8},{10,11... | collective-permute-start | bytes 3538952 | tf_op jit(solution)/shard_map/ppermute | solution.py:58
  91.0 37.5 %collective-permute-start.16 = (bf16[1536,384]{1,0:T(8,128)(2,1)}, bf16[1536,384]{1,0:T(8,128)(2,1)}, u32[]{:S(2)}, u32[]{:S(2)}) collective-permute-start(bf16[1536,384]{1,0:T(8,128)(2,1)} %collective-permute-done.11.refs_8_), channel_id=1, source_target_pairs={{0,1},{1,0},{2,3},{3,2},{4,5},{5,4},{6,7},{7,6},{8,9},{9,8},{10,11... | collective-permute-start | bytes 3538952 | tf_op jit(solution)/shard_map/ppermute | solution.py:58
  93.6 34.9 %collective-permute-start.17 = (bf16[768,384]{1,0:T(8,128)(2,1)S(1)}, bf16[768,384]{1,0:T(8,128)(2,1)S(1)}, u32[]{:S(2)}, u32[]{:S(2)}) collective-permute-start(bf16[768,384]{1,0:T(8,128)(2,1)S(1)} %collective-permute-done.12.refs_9_), channel_id=1, source_target_pairs={{0,1},{1,0},{2,3},{3,2},{4,5},{5,4},{6,7},{7,6},{8,9},{9,8},{10,11... | collective-permute-start | bytes 1769480 | tf_op jit(solution)/shard_map/ppermute | solution.py:58
  94.9 33.5 %collective-permute-start.18 = (bf16[768,384]{1,0:T(8,128)(2,1)}, bf16[768,384]{1,0:T(8,128)(2,1)S(1)}, u32[]{:S(2)}, u32[]{:S(2)}) collective-permute-start(bf16[768,384]{1,0:T(8,128)(2,1)} %collective-permute-done.13.refs_10_), channel_id=1, source_target_pairs={{0,1},{1,0},{2,3},{3,2},{4,5},{5,4},{6,7},{7,6},{8,9},{9,8},{10,11... | collective-permute-start | bytes 1769480 | tf_op jit(solution)/shard_map/ppermute | solution.py:58
  193.6 67.1 %collective-permute-start.27 = (bf16[2,2,768,768]{3,2,1,0:T(8,128)(2,1)}, bf16[2,2,768,768]{3,2,1,0:T(8,128)(2,1)}, u32[]{:S(2)}, u32[]{:S(2)}) collective-permute-start(bf16[2,2,768,768]{3,2,1,0:T(8,128)(2,1)} %get-tuple-element.41), channel_id=1, source_target_pairs={{0,1},{1,0},{2,3},{3,2},{4,5},{5,4},{6,7},{7,6},{8,9},{9,8},{10,11... | collective-permute-start | bytes 14155784 | tf_op jit(solution)/shard_map/ppermute | solution.py:58
  227.0 19.5 %collective-permute-start.19 = (bf16[1536,768]{1,0:T(8,128)(2,1)}, bf16[1536,768]{1,0:T(8,128)(2,1)S(1)}, u32[]{:S(2)}, u32[]{:S(2)}) collective-permute-start(bf16[1536,768]{1,0:T(8,128)(2,1)} %shard_map.221), channel_id=1, source_target_pairs={{0,1},{1,0},{2,3},{3,2},{4,5},{5,4},{6,7},{7,6},{8,9},{9,8},{10,11... | collective-permute-start | bytes 7077896 | tf_op jit(solution)/shard_map/ppermute | solution.py:58
  266.3 40.8 %collective-permute-start.30 = (bf16[2,384,768]{2,1,0:T(8,128)(2,1)S(1)}, bf16[2,384,768]{2,1,0:T(8,128)(2,1)S(1)}, u32[]{:S(2)}, u32[]{:S(2)}) collective-permute-start(bf16[2,384,768]{2,1,0:T(8,128)(2,1)S(1)} %fusion.1), channel_id=1, source_target_pairs={{0,16},{16,0},{1,17},{17,1},{2,18},{18,2},{3,19},{19,3},{4,20},{20... | collective-permute-start | bytes 3538952 | tf_op jit(solution)/shard_map/ppermute | solution.py:58
  268.0 39.9 %collective-permute-start.28 = (bf16[1,768,768]{2,1,0:T(8,128)(2,1)S(1)}, bf16[1,768,768]{2,1,0:T(8,128)(2,1)S(1)}, u32[]{:S(2)}, u32[]{:S(2)}) collective-permute-start(bf16[1,768,768]{2,1,0:T(8,128)(2,1)S(1)} %fusion.2), channel_id=1, source_target_pairs={{0,2},{1,3},{2,0},{3,1},{4,6},{5,7},{6,4},{7,5},{8,10},{9,11},{10,... | collective-permute-start | bytes 3538952 | tf_op jit(solution)/shard_map/ppermute | solution.py:58
  275.7 31.4 %collective-permute-start.23 = (bf16[2,1,192,384]{3,2,1,0:T(8,128)(2,1)S(1)}, bf16[2,1,192,384]{3,2,1,0:T(8,128)(2,1)S(1)}, u32[]{:S(2)}, u32[]{:S(2)}) collective-permute-start(bf16[2,1,192,384]{3,2,1,0:T(8,128)(2,1)S(1)} %slice.175), channel_id=1, source_target_pairs={{0,2},{1,3},{2,0},{3,1},{4,6},{5,7},{6,4},{7,5},{8,10},{9,11},{10,... | collective-permute-start | bytes 884744 | tf_op jit(solution)/shard_map/ppermute | solution.py:58
  276.5 33.3 %collective-permute-start.21 = (bf16[2,1,192,384]{3,2,1,0:T(8,128)(2,1)S(1)}, bf16[2,1,192,384]{3,2,1,0:T(8,128)(2,1)S(1)}, u32[]{:S(2)}, u32[]{:S(2)}) collective-permute-start(bf16[2,1,192,384]{3,2,1,0:T(8,128)(2,1)S(1)} %dynamic-slice_convert_fusion.3), channel_id=1, source_target_pairs={{0,16},{16,0},{1,17},{17,1},{2,18},{18,2},{3,19},{19,3},{4,20},{20... | collective-permute-start | bytes 884744 | tf_op jit(solution)/shard_map/ppermute | solution.py:58
  310.8 36.9 %collective-permute-start.24 = (bf16[384,384]{1,0:T(8,128)(2,1)}, bf16[384,384]{1,0:T(8,128)(2,1)S(1)}, u32[]{:S(2)}, u32[]{:S(2)}) collective-permute-start(bf16[384,384]{1,0:T(8,128)(2,1)} %fusion.9), channel_id=1, source_target_pairs={{0,4},{4,0},{8,12},{12,8},{1,5},{5,1},{9,13},{13,9},{2,6},{6,2},{1... | collective-permute-start | bytes 884744 | tf_op jit(solution)/shard_map/ppermute | solution.py:58
  323.8 19.0 %collective-permute-start.32 = (bf16[384,768]{1,0:T(8,128)(2,1)}, bf16[384,768]{1,0:T(8,128)(2,1)}, u32[]{:S(2)}, u32[]{:S(2)}) collective-permute-start(bf16[384,768]{1,0:T(8,128)(2,1)} %fusion.4), channel_id=1, source_target_pairs={{0,4},{4,0},{8,12},{12,8},{1,5},{5,1},{9,13},{13,9},{2,6},{6,2},{1... | collective-permute-start | bytes 1769480 | tf_op jit(solution)/shard_map/ppermute | solution.py:58
  345.1 41.5 %collective-permute-start.33 = (bf16[384,768]{1,0:T(8,128)(2,1)}, bf16[384,768]{1,0:T(8,128)(2,1)}, u32[]{:S(2)}, u32[]{:S(2)}) collective-permute-start(bf16[384,768]{1,0:T(8,128)(2,1)} %fusion.17), channel_id=1, source_target_pairs={{0,8},{4,12},{8,0},{12,4},{1,9},{5,13},{9,1},{13,5},{2,10},{6,14},... | collective-permute-start | bytes 1769480 | tf_op jit(solution)/shard_map/ppermute | solution.py:58
  349.3 35.9 %collective-permute-start.25 = (bf16[384,384]{1,0:T(8,128)(2,1)}, bf16[384,384]{1,0:T(8,128)(2,1)}, u32[]{:S(2)}, u32[]{:S(2)}) collective-permute-start(bf16[384,384]{1,0:T(8,128)(2,1)} %fusion.16), channel_id=1, source_target_pairs={{0,8},{4,12},{8,0},{12,4},{1,9},{5,13},{9,1},{13,5},{2,10},{6,14},... | collective-permute-start | bytes 884744 | tf_op jit(solution)/shard_map/ppermute | solution.py:58
  366.5 23.9 %collective-permute-start.39 = (f32[8,768]{1,0:T(8,128)S(1)}, f32[8,768]{1,0:T(8,128)S(1)}, u32[]{:S(2)}, u32[]{:S(2)}) collective-permute-start(f32[8,768]{1,0:T(8,128)S(1)} %add.105), channel_id=1, source_target_pairs={{0,8},{4,12},{8,0},{12,4},{1,9},{5,13},{9,1},{13,5},{2,10},{6,14},... | collective-permute-start | bytes 73736 | tf_op jit(solution)/shard_map/ppermute | solution.py:58
  388.4 19.7 %collective-permute-start.34 = (bf16[384,768]{1,0:T(8,128)(2,1)S(1)}, bf16[384,768]{1,0:T(8,128)(2,1)S(1)}, u32[]{:S(2)}, u32[]{:S(2)}) collective-permute-start(bf16[384,768]{1,0:T(8,128)(2,1)S(1)} %get-tuple-element.60), channel_id=1, source_target_pairs={{0,4},{4,0},{8,12},{12,8},{1,5},{5,1},{9,13},{13,9},{2,6},{6,2},{1... | collective-permute-start | bytes 1769480 | tf_op jit(solution)/shard_map/ppermute | solution.py:58
  (34 other events, 414.0 us)
